TPU v7x, 32 devices: a whole 2x2x4 slice. The times are simulated.
32 devices in a mesh: dp: 8 (over z, y), tensor: 4 (over x, core).
Axes of the slice: x: 2, y: 2, z: 4, core: 2. Of those that a mesh axis runs over, the one named last changes fastest.
Arguments:
- inputs: bfloat16 [8192, 2048], P('dp'), may hold values from -6 to 6
- teacher: bfloat16 [8192, 2048], P('dp', 'tensor'), may hold values from -6 to 6
- lengths: int32 [8], P('dp'), may hold values from 213 to 1024, as said below
- gain_one: float32 [2048], replicated, may hold values from 0.5 to 1.5
- w_query_down: bfloat16 [2048, 1024], P(None, 'tensor'), may hold values from -0.125 to 0.125
- gain_query: float32 [1024], replicated, may hold values from 0.5 to 1.5
- w_query_up: bfloat16 [1024, 4096], P(None, 'tensor'), may hold values from -0.375 to 0.375
- w_keyvalue: bfloat16 [2048, 512], replicated, may hold values from -0.125 to 0.125
- w_output: bfloat16 [4096, 2048], P('tensor'), may hold values from -0.75 to 0.75
- gain_two: float32 [2048], replicated, may hold values from 0.5 to 1.5
- w_gate: bfloat16 [2048, 5632], P(None, 'tensor'), may hold values from -0.125 to 0.125
- w_up: bfloat16 [2048, 5632], P(None, 'tensor'), may hold values from -0.125 to 0.125
- w_down: bfloat16 [5632, 2048], P('tensor'), may hold values from -0.078125 to 0.078125
Outputs:
- output: bfloat16 [8192, 2048], P('dp', 'tensor')
- layer_loss: float32 [], replicated
- input_grad: bfloat16 [8192, 2048], P('dp', 'tensor')
- grad_gain_one: float32 [2048], P('tensor')
- grad_w_query_down: float32 [2048, 1024], P(None, 'tensor')
- grad_gain_query: float32 [1024], P('tensor')
- grad_w_query_up: float32 [1024, 4096], P(None, 'tensor')
- grad_w_keyvalue: float32 [2048, 512], P(None, 'tensor')
- grad_w_output: float32 [4096, 2048], P('tensor')
- grad_gain_two: float32 [2048], P('tensor')
- grad_w_gate: float32 [2048, 5632], P(None, 'tensor')
- grad_w_up: float32 [2048, 5632], P(None, 'tensor')
- grad_w_down: float32 [5632, 2048], P('tensor')
Inputs may be any that keep to these rules, and one draw needn't show every extreme that they name: `lengths`: valid tokens fill the first slots of their sequence; the last sequence has all 1024.
All inputs are finite; a program needn't handle non-finite values.
Results may differ from a plain program's by a relative error of at most 0.03.
Values may be sent and summed in bfloat16 or wider, within the bound.
A program may use at most 256 MiB of HBM per device.

v0:
```python
import math

import jax
import jax.numpy as jnp
from jax import lax
from jax.sharding import PartitionSpec as P

epsilon = 1e-05
masked_score = -1e30


def rope_angles(positions, pair_index, head_dim):
    frequency = jnp.exp(-math.log(10000.0) * (2.0 / head_dim) * pair_index)
    angles = positions[:, None] * frequency[None, :]
    return (jnp.cos(angles), jnp.sin(angles))


def rotate_pairs(values, cosines, sines):
    paired = values.reshape(values.shape[:-1] + (values.shape[-1] // 2, 2))
    even_part = paired[..., 0]
    odd_part = paired[..., 1]
    turned = jnp.stack(
        [even_part * cosines - odd_part * sines, even_part * sines + odd_part * cosines], axis=-1
    )
    return turned.reshape(values.shape)


def spread_latent(latent_rows):
    return lax.all_gather(latent_rows, "tensor", axis=1, tiled=True)


def causal_mask(offset, block_rows, seq_len, key_live):
    query_pos = offset + jnp.arange(block_rows)
    causal = query_pos[:, None] >= jnp.arange(seq_len)[None, :]
    return causal[None, None] & key_live[:, None, None, :]


def local(
    inputs,
    teacher,
    lengths,
    gain_one,
    w_query_down,
    gain_query,
    w_query_up,
    w_keyvalue,
    w_output,
    gain_two,
    w_gate,
    w_up,
    w_down,
):
    groups = lax.axis_size("tensor")
    member = lax.axis_index("tensor")
    tokens, model_width = inputs.shape
    seq_count = lengths.shape[0]
    seq_len = tokens // seq_count
    head_dim = w_keyvalue.shape[1] // 2
    local_heads = w_query_up.shape[1] // head_dim
    rank_local = w_query_down.shape[1]
    rank_full = w_query_up.shape[0]
    width_local = model_width // groups
    keyvalue_local = 2 * head_dim // groups
    block_rows = min(512, seq_len)
    score_scale = 1.0 / math.sqrt(head_dim)
    positions = jnp.arange(seq_len, dtype=jnp.float32)
    cosines, sines = rope_angles(positions, jnp.arange(head_dim // 2, dtype=jnp.float32), head_dim)
    key_live = jnp.arange(seq_len)[None, :] < lengths[:, None]
    valid_rows = key_live.reshape(tokens, 1)
    inputs_f = inputs.astype(jnp.float32)
    inverse_one = lax.rsqrt(jnp.mean(inputs_f * inputs_f, axis=-1, keepdims=True) + epsilon)
    normed = (gain_one * inputs_f * inverse_one).astype(jnp.bfloat16)
    latent = jnp.dot(normed, w_query_down, preferred_element_type=jnp.float32).astype(jnp.bfloat16)
    latent_f = latent.astype(jnp.float32)
    gain_slice = lax.dynamic_slice_in_dim(gain_query, member * rank_local, rank_local)
    squares = lax.psum(jnp.sum(latent_f * latent_f, axis=-1), "tensor")
    inverse_query = lax.rsqrt(squares / rank_full + epsilon)[:, None]
    latent_normed = spread_latent((gain_slice * latent_f * inverse_query).astype(jnp.bfloat16))
    query_pre = jnp.dot(latent_normed, w_query_up, preferred_element_type=jnp.float32)
    query_rows = rotate_pairs(
        query_pre.reshape(seq_count, seq_len, local_heads, head_dim),
        cosines[None, :, None, :],
        sines[None, :, None, :],
    ).astype(jnp.bfloat16)
    keyvalue_pre = jnp.dot(normed, w_keyvalue, preferred_element_type=jnp.float32).reshape(
        seq_count, seq_len, 2 * head_dim
    )
    key_rows = rotate_pairs(keyvalue_pre[..., :head_dim], cosines[None], sines[None]).astype(
        jnp.bfloat16
    )
    value_rows = keyvalue_pre[..., head_dim:].astype(jnp.bfloat16)
    contexts = []
    log_totals = []
    for offset in range(0, seq_len, block_rows):
        query_block = query_rows[:, offset : offset + block_rows]
        allowed = causal_mask(offset, block_rows, seq_len, key_live)
        scores = (
            jnp.einsum("sqhd,skd->shqk", query_block, key_rows, preferred_element_type=jnp.float32)
            * score_scale
        )
        scores = jnp.where(allowed, scores, masked_score)
        row_peak = jnp.max(scores, axis=-1, keepdims=True)
        weights = jnp.exp(scores - row_peak)
        totals = jnp.sum(weights, axis=-1, keepdims=True)
        probability = (weights / totals).astype(jnp.bfloat16)
        log_totals.append(row_peak + jnp.log(totals))
        contexts.append(
            jnp.einsum(
                "shqk,skd->sqhd", probability, value_rows, preferred_element_type=jnp.float32
            )
        )
    context = (
        jnp.concatenate(contexts, axis=1)
        .reshape(tokens, local_heads * head_dim)
        .astype(jnp.bfloat16)
    )
    attention_sum = lax.psum(
        jnp.dot(context, w_output, preferred_element_type=jnp.float32).astype(jnp.bfloat16),
        "tensor",
    ).astype(jnp.float32)
    residual = inputs_f + attention_sum
    inverse_two = lax.rsqrt(jnp.mean(residual * residual, axis=-1, keepdims=True) + epsilon)
    normed_two = (gain_two * residual * inverse_two).astype(jnp.bfloat16)
    gate_values = jnp.dot(normed_two, w_gate, preferred_element_type=jnp.float32)
    up_values = jnp.dot(normed_two, w_up, preferred_element_type=jnp.float32)
    sigmoid_gate = jax.nn.sigmoid(gate_values)
    silu_gate = gate_values * sigmoid_gate
    hidden = (silu_gate * up_values).astype(jnp.bfloat16)
    feed_share = lax.psum_scatter(
        jnp.dot(hidden, w_down, preferred_element_type=jnp.float32).astype(jnp.bfloat16),
        "tensor",
        scatter_dimension=1,
        tiled=True,
    ).astype(jnp.float32)
    residual_share = lax.dynamic_slice_in_dim(residual, member * width_local, width_local, 1)
    output = (residual_share + feed_share).astype(jnp.bfloat16)
    differ = jnp.where(valid_rows, output.astype(jnp.float32) - teacher.astype(jnp.float32), 0.0)
    error_sum, valid_count = lax.psum(
        (jnp.sum(differ * differ), jnp.sum(lengths).astype(jnp.float32) / groups), ("dp", "tensor")
    )
    layer_loss = error_sum / (valid_count * model_width)
    grad_share = differ * (float(tokens * lax.axis_size("dp")) / valid_count)
    grad_out = lax.all_gather(grad_share.astype(jnp.bfloat16), "tensor", axis=1, tiled=True).astype(
        grad_share.dtype
    )
    grad_out_low = grad_out.astype(jnp.bfloat16)
    grad_w_down = jnp.einsum("tf,td->fd", hidden, grad_out_low, preferred_element_type=jnp.float32)
    grad_hidden = jnp.einsum("td,fd->tf", grad_out_low, w_down, preferred_element_type=jnp.float32)
    gate_grad = (
        grad_hidden * up_values * sigmoid_gate * (1.0 + gate_values * (1.0 - sigmoid_gate))
    ).astype(jnp.bfloat16)
    up_grad = (grad_hidden * silu_gate).astype(jnp.bfloat16)
    grad_w_gate = jnp.einsum("tk,tf->kf", normed_two, gate_grad, preferred_element_type=jnp.float32)
    grad_w_up = jnp.einsum("tk,tf->kf", normed_two, up_grad, preferred_element_type=jnp.float32)
    normed_two_part = jnp.einsum(
        "tf,kf->tk", gate_grad, w_gate, preferred_element_type=jnp.float32
    ) + jnp.einsum("tf,kf->tk", up_grad, w_up, preferred_element_type=jnp.float32)
    grad_normed_two = lax.psum(normed_two_part.astype(jnp.bfloat16), "tensor").astype(jnp.float32)
    scaled_two = gain_two * grad_normed_two
    grad_residual = (
        grad_out
        + inverse_two * scaled_two
        - residual * inverse_two**3 * jnp.mean(scaled_two * residual, axis=-1, keepdims=True)
    )
    grad_gain_two = lax.dynamic_slice_in_dim(
        jnp.sum(grad_normed_two * residual * inverse_two, axis=0), member * width_local, width_local
    )
    grad_residual_low = grad_residual.astype(jnp.bfloat16)
    residual_grad_share = lax.dynamic_slice_in_dim(
        grad_residual, member * width_local, width_local, 1
    )
    grad_w_output = jnp.einsum(
        "tc,td->cd", context, grad_residual_low, preferred_element_type=jnp.float32
    )
    grad_context = jnp.einsum(
        "td,cd->tc", grad_residual_low, w_output, preferred_element_type=jnp.float32
    ).astype(jnp.bfloat16)
    grad_context = grad_context.reshape(seq_count, seq_len, local_heads, head_dim)
    grad_keys = jnp.zeros((seq_count, seq_len, head_dim), jnp.float32)
    grad_values = jnp.zeros((seq_count, seq_len, head_dim), jnp.float32)
    grad_queries = []
    for number, offset in enumerate(range(0, seq_len, block_rows)):
        query_block = query_rows[:, offset : offset + block_rows]
        allowed = causal_mask(offset, block_rows, seq_len, key_live)
        scores = (
            jnp.einsum("sqhd,skd->shqk", query_block, key_rows, preferred_element_type=jnp.float32)
            * score_scale
        )
        scores = jnp.where(allowed, scores, masked_score)
        probability = jnp.where(allowed, jnp.exp(scores - log_totals[number]), 0.0)
        grad_block = grad_context[:, offset : offset + block_rows]
        grad_probs = jnp.einsum(
            "sqhd,skd->shqk", grad_block, value_rows, preferred_element_type=jnp.float32
        )
        inner = jnp.sum(probability * grad_probs, axis=-1, keepdims=True)
        grad_scores = (score_scale * probability * (grad_probs - inner)).astype(jnp.bfloat16)
        grad_queries.append(
            jnp.einsum("shqk,skd->sqhd", grad_scores, key_rows, preferred_element_type=jnp.float32)
        )
        grad_keys = grad_keys + jnp.einsum(
            "shqk,sqhd->skd", grad_scores, query_block, preferred_element_type=jnp.float32
        )
        grad_values = grad_values + jnp.einsum(
            "shqk,sqhd->skd",
            probability.astype(jnp.bfloat16),
            grad_block,
            preferred_element_type=jnp.float32,
        )
    grad_query_rows = jnp.concatenate(grad_queries, axis=1)
    grad_query_pre = (
        rotate_pairs(grad_query_rows, cosines[None, :, None, :], -sines[None, :, None, :])
        .reshape(tokens, local_heads * head_dim)
        .astype(jnp.bfloat16)
    )
    grad_w_query_up = jnp.einsum(
        "tr,tc->rc", latent_normed, grad_query_pre, preferred_element_type=jnp.float32
    )
    keyvalue_part = jnp.concatenate([grad_keys, grad_values], axis=-1).reshape(tokens, 2 * head_dim)
    latent_part = jnp.einsum(
        "tc,rc->tr", grad_query_pre, w_query_up, preferred_element_type=jnp.float32
    )
    keyvalue_share, latent_share = (
        lax.psum_scatter(
            keyvalue_part.astype(jnp.bfloat16), "tensor", scatter_dimension=1, tiled=True
        ).astype(jnp.float32),
        lax.psum_scatter(
            latent_part.astype(jnp.bfloat16), "tensor", scatter_dimension=1, tiled=True
        ).astype(jnp.float32),
    )
    pair_global = member * (keyvalue_local // 2) + jnp.arange(keyvalue_local // 2)
    pair_keys = pair_global < head_dim // 2
    slice_cos, slice_sin = rope_angles(
        positions, (pair_global % (head_dim // 2)).astype(jnp.float32), head_dim
    )
    keyvalue_seq = keyvalue_share.reshape(seq_count, seq_len, keyvalue_local)
    turned = rotate_pairs(keyvalue_seq, slice_cos[None], -slice_sin[None])
    grad_keyvalue = (
        jnp.where(jnp.repeat(pair_keys, 2)[None, None, :], turned, keyvalue_seq)
        .reshape(tokens, keyvalue_local)
        .astype(jnp.bfloat16)
    )
    w_keyvalue_share = lax.dynamic_slice_in_dim(
        w_keyvalue, member * keyvalue_local, keyvalue_local, 1
    )
    grad_w_keyvalue = jnp.einsum(
        "tk,tc->kc", normed, grad_keyvalue, preferred_element_type=jnp.float32
    )
    scaled_latent = gain_slice * latent_share
    grad_gain_query = jnp.sum(latent_share * latent_f * inverse_query, axis=0)
    latent_dots = lax.psum(jnp.sum(scaled_latent * latent_f, axis=-1), "tensor")
    grad_latent = (
        inverse_query * scaled_latent
        - latent_f * inverse_query**3 * (latent_dots / rank_full)[:, None]
    ).astype(jnp.bfloat16)
    grad_w_query_down = jnp.einsum(
        "tk,tr->kr", normed, grad_latent, preferred_element_type=jnp.float32
    )
    normed_part = jnp.einsum(
        "tr,kr->tk", grad_latent, w_query_down, preferred_element_type=jnp.float32
    ) + jnp.einsum("tc,kc->tk", grad_keyvalue, w_keyvalue_share, preferred_element_type=jnp.float32)
    grad_normed = lax.psum_scatter(
        normed_part.astype(jnp.bfloat16), "tensor", scatter_dimension=1, tiled=True
    ).astype(jnp.float32)
    inputs_share = lax.dynamic_slice_in_dim(inputs_f, member * width_local, width_local, 1)
    gain_share = lax.dynamic_slice_in_dim(gain_one, member * width_local, width_local)
    scaled_one = gain_share * grad_normed
    input_dots = lax.psum(jnp.sum(scaled_one * inputs_share, axis=-1), "tensor")
    grad_gain_one = jnp.sum(grad_normed * inputs_share * inverse_one, axis=0)
    input_grad = (
        residual_grad_share
        + inverse_one * scaled_one
        - inputs_share * inverse_one**3 * (input_dots / model_width)[:, None]
    ).astype(jnp.bfloat16)
    (
        grad_gain_one,
        grad_w_query_down,
        grad_gain_query,
        grad_w_query_up,
        grad_w_keyvalue,
        grad_w_output,
        grad_gain_two,
        grad_w_gate,
        grad_w_up,
        grad_w_down,
    ) = (
        lax.psum(grad_gain_one.astype(jnp.bfloat16), "dp").astype(jnp.float32),
        lax.psum(grad_w_query_down.astype(jnp.bfloat16), "dp").astype(jnp.float32),
        lax.psum(grad_gain_query.astype(jnp.bfloat16), "dp").astype(jnp.float32),
        lax.psum(grad_w_query_up.astype(jnp.bfloat16), "dp").astype(jnp.float32),
        lax.psum(grad_w_keyvalue.astype(jnp.bfloat16), "dp").astype(jnp.float32),
        lax.psum(grad_w_output.astype(jnp.bfloat16), "dp").astype(jnp.float32),
        lax.psum(grad_gain_two.astype(jnp.bfloat16), "dp").astype(jnp.float32),
        lax.psum(grad_w_gate.astype(jnp.bfloat16), "dp").astype(jnp.float32),
        lax.psum(grad_w_up.astype(jnp.bfloat16), "dp").astype(jnp.float32),
        lax.psum(grad_w_down.astype(jnp.bfloat16), "dp").astype(jnp.float32),
    )
    return (
        output,
        layer_loss,
        input_grad,
        grad_gain_one,
        grad_w_query_down,
        grad_gain_query,
        grad_w_query_up,
        grad_w_keyvalue,
        grad_w_output,
        grad_gain_two,
        grad_w_gate,
        grad_w_up,
        grad_w_down,
    )


def solution(mesh):
    placed = (
        P("dp", None),
        P("dp", "tensor"),
        P("dp"),
        P(),
        P(None, "tensor"),
        P(),
        P(None, "tensor"),
        P(),
        P("tensor", None),
        P(),
        P(None, "tensor"),
        P(None, "tensor"),
        P("tensor", None),
    )
    return jax.shard_map(
        local,
        mesh=mesh,
        in_specs=placed,
        out_specs=(
            P("dp", "tensor"),
            P(),
            P("dp", "tensor"),
            P("tensor"),
            P(None, "tensor"),
            P("tensor"),
            P(None, "tensor"),
            P(None, "tensor"),
            P("tensor", None),
            P("tensor"),
            P(None, "tensor"),
            P(None, "tensor"),
            P("tensor", None),
        ),
        check_vma=False,
    )
```

profile of v0, /device:TPU:0, one launch (start us, length us, event | category | flops | bytes accessed | tf_op | source)
XLA Modules:
  0.0 1462.0 jit_solution(2972834171248635868)
XLA Ops:
  13.9 8.4 psum.119
  25.9 4.7 convolution_bitcast_fusion.2
  48.2 6.6 fusion.128
  54.8 5.8 reshape_reshape.7
  60.7 7.4 subtract_convert_fusion.1
  68.1 5.1 pad_maximum_fusion.1
  103.6 6.2 convolution_convert_fusion.5
  109.9 85.6 %all-reduce.7.cloned.1.call-done = bf16[1024,2048]{1,0:T(8,128)(2,1)} async-done(((bf16[1024,2048]{1,0:T(8,128)(2,1)}), bf16[1024,2048]{1,0:T(8,128)(2,1)}) %all-reduce.7.cloned.1.call-update) | async-done | bytes 4194320 | tf_op jit(solution)/shard_map/psum | solution.py:117
  195.5 8.3 convert_add_fusion
  206.7 10.8 fusion.129
  217.5 8.7 multiply_convert_fusion.4
  227.8 8.2 convolution_convert_fusion.3
  236.1 44.6 %reduce-scatter.5.cloned.1.call-done = bf16[1024,512]{1,0:T(8,128)(2,1)} async-done(((bf16[1024,2048]{1,0:T(8,128)(2,1)}), bf16[1024,512]{1,0:T(8,128)(2,1)}) %reduce-scatter.5.cloned.1.call-update) | async-done | bytes 1048592 | tf_op jit(solution)/shard_map/reduce_scatter | solution.py:129
  280.7 4.3 multiply_reduce_fusion.2
  285.0 39.5 %all-reduce = (f32[]{:T(128)}, f32[]{:T(128)}) all-reduce(f32[]{:T(128)} %get-tuple-element.31, f32[]{:T(128)S(6)} %div.55), channel_id=1, replica_groups=mesh['dp'=8,'tensor'=4] {'dp','tensor'}, use_global_device_ids=true, to_apply=%region_11.12 | all-reduce | flops 2 | bytes 16 | tf_op jit(solution)/shard_map/psum | solution.py:138
  328.2 35.5 %all-gather.5.cloned.1.call-done = bf16[1024,2048]{1,0:T(8,128)(2,1)} async-done(((bf16[1024,512]{1,0:T(8,128)(2,1)}), bf16[1024,2048]{1,0:T(8,128)(2,1)}) %all-gather.5.cloned.1.call-update) | async-done | bytes 4194320 | tf_op jit(solution)/shard_map/all_gather | solution.py:143
  363.6 14.3 multiply_convert_fusion.2
  378.0 10.8 fusion.130
  388.8 11.0 add_convert_fusion.1
  401.9 83.6 %all-reduce.9.cloned.1.call-done = bf16[1024,2048]{1,0:T(8,128)(2,1)} async-done(((bf16[1024,2048]{1,0:T(8,128)(2,1)}), bf16[1024,2048]{1,0:T(8,128)(2,1)}) %all-reduce.9.cloned.1.call-update) | async-done | bytes 4194320 | tf_op jit(solution)/shard_map/psum | solution.py:158
  485.5 8.4 fusion.6
  493.9 5.2 fusion.3
  499.2 10.0 fusion.49
  511.0 4.6 fusion.10
  515.7 4.6 fusion.7
  522.0 16.8 %fusion.24 = (bf16[4,512,1024]{1,2,0:T(8,128)(2,1)}, bf16[4,512,1024]{1,2,0:T(8,128)(2,1)}) fusion(f32[1024,512,4]{1,0,2:T(8,128)} %get-tuple-element.73, f32[1,4,512,1024]{2,3,1,0:T(8,128)} %copy-done.6, f32[4,512]{1,0:T(4,128)S(1)} %get-tuple-element.72, f32[4,512]{1,0:T(4,128)S(1)} %log_add_fusion.1, pred[512,1024]{0,1:T(8,128)(4,1)S(1)} %get-tuple-element.57, ...), kind=kLoop, calls=%fused_computation.50 | loop fusion | flops 25165824 | bytes 43024384 | tf_op jit(solution)/shard_map/reshape.58
  550.1 4.8 pad_maximum_fusion
  554.9 6.2 reshape.677
  561.1 7.4 subtract_convert_fusion
  568.5 5.6 pad_maximum_fusion.3
  578.3 5.9 convolution_convert_fusion.8
  588.4 4.9 fusion.101
  593.2 22.1 %reduce-scatter.7.cloned.1.call-done = bf16[1024,256]{0,1:T(8,128)(2,1)} async-done(((bf16[1024,1024]{0,1:T(8,128)(2,1)}), bf16[1024,256]{0,1:T(8,128)(2,1)}) %reduce-scatter.7.cloned.1.call-update) | async-done | bytes 524304 | tf_op jit(solution)/shard_map/reduce_scatter | solution.py:226
  616.9 5.8 psum.124
  622.6 7.4 add_convert_fusion
  630.2 10.6 convolution_convert_fusion
  640.8 8.7 convolution_convert_fusion.2
  649.5 8.7 convolution_convert_fusion.1
  661.9 6.2 convolution_convert_fusion.4
  673.8 6.7 convert_element_type.238
  684.8 22.8 %all-reduce.1 = (bf16[512]{0:T(512)(128)(2,1)S(1)}, bf16[256]{0:T(256)(128)(2,1)S(1)}, bf16[512]{0:T(512)(128)(2,1)S(1)}) all-reduce(bf16[512]{0:T(512)(128)(2,1)S(1)} %get-tuple-element.15, bf16[256]{0:T(256)(128)(2,1)S(1)} %get-tuple-element.17, bf16[512]{0:T(512)(128)(2,1)S(1)} %dynamic_slice.36), channel_id=1, replica_groups=mesh['dp'=8,'tensor'=4] {'dp'}, use_global_device_ids=true, to_apply=%region_25.26 | all-reduce | flops 1280 | bytes 5120 | tf_op jit(solution)/shard_map/psum | solution.py:286
  709.3 6.0 psum.125
  715.3 4.2 fusion.40
  719.5 706.0 %all-reduce.11.cloned.1.call-done = (bf16[2048,256]{1,0:T(8,128)(2,1)}, bf16[1024,1024]{1,0:T(8,128)(2,1)}, bf16[2048,128]{1,0:T(8,128)(2,1)}, bf16[1024,2048]{1...) async-done(((bf16[2048,256]{1,0:T(8,128)(2,1)}, bf16[1024,1024]{1,0:T(8,128)(2,1)}, ...) | async-done | bytes 25165840 | tf_op jit(solution)/shard_map/psum | solution.py:287
  1432.2 5.1 convert_element_type.292
  1437.4 5.6 convert_element_type.296
  1443.0 5.2 convert_element_type.298
  1448.2 6.0 convert_element_type.300
  (250 shorter events, 112.3 us)
Async XLA Ops:
  7.2 18.7 %copy-start = (bf16[2048,512]{1,0:T(8,128)(2,1)S(1)}, bf16[2048,512]{1,0:T(8,128)(2,1)}, u32[]{:S(2)}) copy-start(bf16[2048,512]{1,0:T(8,128)(2,1)} %param.20) | copy-start | bytes 6291460
  7.2 41.0 %all-gather.3.cloned.1.call-start = ((), (), s32[]{:S(2)}) async-start(), calls=%async_computation.4 | async-start | bytes 2621440 | tf_op jit(solution)/shard_map/all_gather | solution.py:29
  11.1 14.8 %copy-start.43 = (f32[1024]{0:T(1024)}, f32[1024]{0:T(1024)S(1)}, u32[]{:S(2)}) copy-start(f32[1024]{0:T(1024)S(1)} %get-tuple-element.52) | copy-start | bytes 12292
  13.9 16.7 %copy-start.18 = (bf16[1024,256]{0,1:T(8,128)(2,1)}, bf16[1024,256]{0,1:T(8,128)(2,1)S(1)}, u32[]{:S(2)}) copy-start(bf16[1024,256]{0,1:T(8,128)(2,1)S(1)} %get-tuple-element.63) | copy-start | bytes 1572868
  22.9 7.7 copy-start.41
  25.2 170.3 %all-reduce.7.cloned.1.call-start = ((), (), s32[]{:S(2)}) async-start(), calls=%async_computation.5 | async-start | bytes 8388608 | tf_op jit(solution)/shard_map/psum | solution.py:117
  47.4 32.9 %copy-start.11 = (pred[512,1024]{0,1:T(8,128)(4,1)}, pred[512,1024]{0,1:T(8,128)(4,1)S(1)}, u32[]{:S(2)}) copy-start(pred[512,1024]{0,1:T(8,128)(4,1)S(1)} %get-tuple-element.58) | copy-start | bytes 1572868
  109.8 94.0 %copy-start.40 = (f32[2048]{0:T(1024)S(1)}, f32[2048]{0:T(1024)}, u32[]{:S(2)}) copy-start(f32[2048]{0:T(1024)} %param.22) | copy-start | bytes 24580
  109.8 170.9 %reduce-scatter.5.cloned.1.call-start = ((), (), s32[]{:S(2)}) async-start(), calls=%async_computation.6 | async-start | bytes 5242880 | tf_op jit(solution)/shard_map/reduce_scatter | solution.py:129
  195.5 8.3 copy-start.2
  195.5 8.4 copy-start.7
  203.8 13.6 slice-start.14
  206.7 10.8 copy-start.22
  206.7 10.8 slice-start.15
  206.7 21.1 %slice-start.12 = ((s8[5767168]{0:T(1024)(128)(4,1)}), s8[4194304]{0:T(1024)(128)(4,1)S(1)}, s32[]{:S(2)}) async-start(s8[5767168]{0:T(1024)(128)(4,1)} %bitcast.242), calls=%async_computation.25 | async-start | bytes 8388608
  217.5 8.7 copy-start.54
  217.5 10.3 slice-start.13
  236.0 127.6 %all-gather.5.cloned.1.call-start = ((), (), s32[]{:S(2)}) async-start(), calls=%async_computation.7 | async-start | bytes 5242880 | tf_op jit(solution)/shard_map/all_gather | solution.py:143
  328.1 157.4 %all-reduce.9.cloned.1.call-start = ((), (), s32[]{:S(2)}) async-start(), calls=%async_computation.8 | async-start | bytes 8388608 | tf_op jit(solution)/shard_map/psum | solution.py:158
  378.0 10.8 copy-start.55
  378.0 10.8 copy-start.57
  399.8 185.1 %reduce-scatter.9.cloned.1.call-start = ((), (), s32[]{:S(2)}) async-start(), calls=%async_computation.10 | async-start | bytes 1310720 | tf_op jit(solution)/shard_map/reduce_scatter | solution.py:223
  485.5 8.4 copy-start.3
  485.5 8.4 copy-start.8
  485.5 8.4 copy-start.9
  493.9 15.3 %slice-start.2 = ((s8[8388608]{0:T(1024)(128)(4,1)}), s8[4194304]{0:T(1024)(128)(4,1)S(1)}, s32[]{:S(2)}) async-start(s8[8388608]{0:T(1024)(128)(4,1)} %bitcast.225), calls=%async_computation.15 | async-start | bytes 8388608
  499.2 10.1 copy-start.10
  499.2 10.1 slice-start.3
  509.3 6.3 slice-start
  522.0 16.8 %copy-start.34 = (bf16[1,512,4,256]{3,1,2,0:T(8,128)(2,1)S(1)}, bf16[1,512,4,256]{3,1,2,0:T(8,128)(2,1)}, u32[]{:S(2)}) copy-start(bf16[1,512,4,256]{3,1,2,0:T(8,128)(2,1)} %copy.169) | copy-start | bytes 3145732
  550.1 65.3 %reduce-scatter.7.cloned.1.call-start = ((), (), s32[]{:S(2)}) async-start(), calls=%async_computation.9 | async-start | bytes 2621440 | tf_op jit(solution)/shard_map/reduce_scatter | solution.py:226
  584.2 97.9 %reduce-scatter.11.cloned.1.call-start = ((), (), s32[]{:S(2)}) async-start(), calls=%async_computation.11 | async-start | bytes 5242880 | tf_op jit(solution)/shard_map/reduce_scatter | solution.py:261
  588.3 27.1 %copy-start.19 = (bf16[1024,256]{0,1:T(8,128)(2,1)S(1)}, bf16[1024,256]{0,1:T(8,128)(2,1)}, u32[]{:S(2)}) copy-start(bf16[1024,256]{0,1:T(8,128)(2,1)} %copy-done.18) | copy-start | bytes 1572868
  588.3 27.1 %copy-start.42 = (f32[1024]{0:T(1024)S(1)}, f32[1024]{0:T(1024)}, u32[]{:S(2)}) copy-start(f32[1024]{0:T(1024)} %copy-done.41) | copy-start | bytes 12292
  588.4 27.0 %copy-start.46 = (f32[256]{0:T(256)S(1)}, f32[256]{0:T(256)}, u32[]{:S(2)}) copy-start(f32[256]{0:T(256)} %copy-done.45) | copy-start | bytes 3076
  588.4 34.3 %copy-start.48 = (f32[1024]{0:T(1024)S(1)}, f32[1024]{0:T(1024)}, u32[]{:S(2)}) copy-start(f32[1024]{0:T(1024)} %get-tuple-element.53) | copy-start | bytes 12292
  630.1 795.4 %all-reduce.11.cloned.1.call-start = ((), (), s32[]{:S(2)}) async-start(), calls=%async_computation.12 | async-start | bytes 50331648 | tf_op jit(solution)/shard_map/psum | solution.py:287
  630.1 10.6 copy-start.23
  630.2 10.6 copy-start.56
  640.8 8.7 copy-start.58
  640.8 21.1 %slice-start.4 = ((s8[8388608]{0:T(1024)(128)(4,1)}), s8[4194304]{0:T(1024)(128)(4,1)S(1)}, s32[]{:S(2)}) async-start(s8[8388608]{0:T(1024)(128)(4,1)} %bitcast.227), calls=%async_computation.17 | async-start | bytes 8388608
  649.5 8.7 copy-start.32
  649.5 8.7 copy-start.52
  649.5 12.4 slice-start.5
  673.8 41.5 %copy-start.47 = (f32[1024]{0:T(1024)S(1)}, f32[1024]{0:T(1024)}, u32[]{:S(2)}) copy-start(f32[1024]{0:T(1024)} %get-tuple-element.51) | copy-start | bytes 12292
  1428.4 9.0 slice-start.10
  1432.2 10.8 slice-start.8
  1437.4 10.8 slice-start.6
  (36 other events, 131.3 us)
Sparse Core Ops, SparseCore 0:
  25.3 22.8 all-gather.2
  110.0 85.4 all-reduce.6
  236.1 44.5 reduce-scatter.4
  328.2 35.3 all-gather.4
  400.0 85.4 all-reduce.8
  550.2 24.9 reduce-scatter.8
  584.3 31.0 reduce-scatter.6
  630.2 45.0 reduce-scatter.10
  682.3 743.1 all-reduce.10
where the time goes:
time: 1470 us; the launch traced here: 1460 us
  waiting for transfers between devices  978 us (67%)
  matrix products  189 us (13%)
  other arithmetic  141 us (10%)
  blocking collectives  82.5 us (6%)
  local copies, waits for them, and re-layouts  52.3 us (4%)
  between operations  18.8 us (1%)
    psum x1, waiting for transfers between devices, local(): lax.psum(grad_w_query_down.astype(jnp.bfloat16), 'dp').astype(jnp.float32)  706 us
    psum x1, waiting for transfers between devices, local(): lax.psum(jnp.dot(context, w_output, preferred_element_type=jnp.float32).a...  85.6 us
    psum x1, waiting for transfers between devices, local(): lax.psum(normed_two_part.astype(jnp.bfloat16), 'tensor').astype(jnp.float32)  83.6 us
    reduce_scatter x1, waiting for transfers between devices, local(): lax.psum_scatter(jnp.dot(hidden, w_down, preferred_element_type=jnp.float...  44.6 us
    psum x1, blocking collectives, local(): lax.psum((jnp.sum(differ * differ), jnp.sum(lengths).astype(jnp.float32)...  39.5 us
    all_gather x1, waiting for transfers between devices, local(): lax.all_gather(grad_share.astype(jnp.bfloat16), 'tensor', axis=1, tiled=T...  35.5 us
    another operation x4, other arithmetic  33.8 us
  transfers between devices with their start and end apart: 9, of which 7 were waited for; matrix products, arithmetic and copies ran while one was open for 8% of the time, Pallas kernels for 0%

commit v1 on v0

v1 whole, which is shorter than its diff:
```python
import functools
import math

import jax
import jax.numpy as jnp
from jax import lax
from jax.experimental import pallas as pl
from jax.experimental.pallas import tpu as pltpu
from jax.sharding import PartitionSpec as P


epsilon = 1e-05
masked_score = -1e30


def rope_angles(positions, pair_index, head_dim):
    frequency = jnp.exp(-math.log(10000.0) * (2.0 / head_dim) * pair_index)
    angles = positions[:, None] * frequency[None, :]
    return (jnp.cos(angles), jnp.sin(angles))


def dp_layout():
    size = lax.axis_size("dp")
    depth = 4 if size % 4 == 0 else 1
    return depth, size // depth


def split_rows(values, bit):
    half = values.shape[0] // 2
    keep = lax.dynamic_slice_in_dim(values, bit * half, half, 0)
    send = lax.dynamic_slice_in_dim(values, (1 - bit) * half, half, 0)
    return keep, send


def join_rows(mine, theirs, bit):
    first = bit == 0
    return jnp.concatenate(
        [jnp.where(first, mine, theirs), jnp.where(first, theirs, mine)], axis=0
    )


chunk_rows = 64
slots = 8


def grid_place(width):
    index = lax.axis_index("dp")
    level, column = index // width, index % width
    is_end = (level == 0) | (level == 3)
    upper = level // 2
    column_partner = level * width + (1 - column)
    chain_level = jnp.where(is_end, 1 + upper, 3 * upper)
    chain_partner = chain_level * width + column
    middle_partner = (3 - level) * width + column
    return column, upper, is_end, column_partner, chain_partner, middle_partner


def sum_kernel(starts, width, *refs):
    count = len(starts) - 1
    sources, results = refs[:count], refs[count : 2 * count]
    (
        load_a, first_a, sum_a, second_a, third_a, total_a, other_a,
        load_b, first_b, sum_b, second_b, half_b, third_b, total_b, other_b,
        load_sem, store_sem, send_sem, recv_sem,
    ) = refs[2 * count :]
    rounds = starts[-1] // 2
    half = chunk_rows // 2
    column, upper, is_end, column_partner, chain_partner, middle_partner = grid_place(width)
    is_middle = jnp.logical_not(is_end)

    def signal(partner):
        pl.semaphore_signal(
            barrier, inc=1, device_id={"dp": partner}, device_id_type=pl.DeviceIdType.MESH
        )

    barrier = pltpu.get_barrier_semaphore()
    signal(column_partner)
    signal(chain_partner)

    @pl.when(is_middle)
    def _():
        signal(middle_partner)

    pl.semaphore_wait(barrier, jnp.where(is_end, 2, 3))

    def remote(kind, slot, source, target, partner):
        return pltpu.make_async_remote_copy(
            src_ref=source,
            dst_ref=target,
            send_sem=send_sem.at[kind, slot],
            recv_sem=recv_sem.at[kind, slot],
            device_id={"dp": partner},
            device_id_type=pl.DeviceIdType.MESH,
        )

    def load(kind, number, slot, target):
        chunk = 2 * number + kind
        for i in range(count):

            @pl.when((chunk >= starts[i]) & (chunk < starts[i + 1]))
            def _():
                row = pl.multiple_of((chunk - starts[i]) * chunk_rows, chunk_rows)
                pltpu.make_async_copy(
                    sources[i].at[pl.ds(row, chunk_rows)], target.at[slot], load_sem.at[kind, slot]
                ).start()

    def load_wait(kind, slot, target):
        pltpu.make_async_copy(
            sources[0].at[pl.ds(0, chunk_rows)], target.at[slot], load_sem.at[kind, slot]
        ).wait()

    def store(kind, number, slot, bit, mine, theirs):
        chunk = 2 * number + kind
        for i in range(count):

            @pl.when((chunk >= starts[i]) & (chunk < starts[i + 1]))
            def _():
                row = (chunk - starts[i]) * chunk_rows
                for part, (ref, side) in enumerate(((mine, bit), (theirs, 1 - bit))):
                    place = pl.multiple_of(row + side * half, half)
                    pltpu.make_async_copy(
                        ref.at[slot], results[i].at[pl.ds(place, half)], store_sem.at[kind, part, slot]
                    ).start()

    def store_wait(kind, slot, mine, theirs):
        for part, ref in enumerate((mine, theirs)):
            pltpu.make_async_copy(
                ref.at[slot], results[0].at[pl.ds(0, half)], store_sem.at[kind, part, slot]
            ).wait()

    def rows(side):
        return pl.ds(pl.multiple_of(side * half, half), half)

    def plus(left, right):
        return (left.astype(jnp.float32) + right.astype(jnp.float32)).astype(jnp.bfloat16)

    def copy_a1(slot):
        return remote(0, slot, load_a.at[slot, rows(1 - column)], first_a.at[slot], column_partner)

    def copy_a2(slot):
        return remote(1, slot, sum_a.at[slot], second_a.at[slot], chain_partner)

    def copy_a3(slot):
        return remote(2, slot, sum_a.at[slot], third_a.at[slot], middle_partner)

    def copy_a4(slot):
        return remote(3, slot, total_a.at[slot], total_a.at[slot], chain_partner)

    def copy_a5(slot):
        return remote(4, slot, total_a.at[slot], other_a.at[slot], column_partner)

    def copy_b1(slot):
        return remote(5, slot, load_b.at[slot], first_b.at[slot], chain_partner)

    def copy_b2(slot):
        return remote(6, slot, sum_b.at[slot, rows(1 - upper)], second_b.at[slot], middle_partner)

    def copy_b3(slot):
        return remote(7, slot, half_b.at[slot], third_b.at[slot], column_partner)

    def copy_b4(slot):
        return remote(8, slot, total_b.at[slot], other_b.at[slot], middle_partner)

    def copy_b5(slot):
        return remote(9, slot, total_b.at[slot], total_b.at[slot], chain_partner)

    def copy_b6(slot):
        return remote(10, slot, other_b.at[slot], other_b.at[slot], chain_partner)

    def stage(number, body):
        @pl.when((number >= 0) & (number < rounds))
        def _():
            body(number, lax.rem(number + slots, slots))

    def stage_6(number, slot):
        store_wait(0, slot, total_a, other_a)
        store_wait(1, slot, total_b, other_b)

    def stage_5(number, slot):
        copy_a5(slot).wait_recv()
        copy_a1(slot).wait_send()
        copy_a5(slot).wait_send()

        @pl.when(is_end)
        def _():
            copy_b5(slot).wait_recv()
            copy_b6(slot).wait_recv()
            copy_a2(slot).wait_send()
            copy_b1(slot).wait_send()

        @pl.when(is_middle)
        def _():
            copy_a3(slot).wait_send()
            copy_a4(slot).wait_send()
            copy_b2(slot).wait_send()
            copy_b3(slot).wait_send()
            copy_b4(slot).wait_send()
            copy_b5(slot).wait_send()
            copy_b6(slot).wait_send()

        store(0, number, slot, column, total_a, other_a)
        store(1, number, slot, upper, total_b, other_b)

    def stage_4(number, slot):
        @pl.when(is_end)
        def _():
            copy_a4(slot).wait_recv()
            copy_a5(slot).start()

        @pl.when(is_middle)
        def _():
            copy_b4(slot).wait_recv()
            copy_b6(slot).start()

    def stage_3(number, slot):
        @pl.when(is_middle)
        def _():
            copy_a3(slot).wait_recv()
            total_a[slot] = plus(sum_a[slot], third_a[slot])
            copy_a4(slot).start()
            copy_a5(slot).start()
            copy_b3(slot).wait_recv()
            total_b[slot] = plus(half_b[slot], third_b[slot])
            copy_b4(slot).start()
            copy_b5(slot).start()

    def stage_2(number, slot):
        @pl.when(is_middle)
        def _():
            copy_a2(slot).wait_recv()
            sum_a[slot] = plus(sum_a[slot], second_a[slot])
            copy_a3(slot).start()
            copy_b2(slot).wait_recv()
            half_b[slot] = plus(sum_b[slot, rows(upper)], second_b[slot])
            copy_b3(slot).start()

    def stage_1(number, slot):
        copy_a1(slot).wait_recv()
        sum_a[slot] = plus(load_a[slot, rows(column)], first_a[slot])

        @pl.when(is_end)
        def _():
            copy_a2(slot).start()

        @pl.when(is_middle)
        def _():
            copy_b1(slot).wait_recv()
            sum_b[slot] = plus(load_b[slot], first_b[slot])
            copy_b2(slot).start()

    def stage_0(number, slot):
        load_wait(0, slot, load_a)
        copy_a1(slot).start()
        load_wait(1, slot, load_b)

        @pl.when(is_end)
        def _():
            copy_b1(slot).start()

    def prefetch(number, slot):
        load(0, number, slot, load_a)
        load(1, number, slot, load_b)

    prefetch(0, 0)
    stages = (stage_0, stage_1, stage_2, stage_3, stage_4, stage_5, stage_6)

    def step(number, carry):
        for late in range(len(stages) - 1, -1, -1):
            stage(number - late, stages[late])
        stage(number + 1, prefetch)
        return carry

    lax.fori_loop(0, rounds + len(stages) - 1, step, 0)


def kernel_sum(arrays):
    width = dp_layout()[1]
    starts = [0]
    for values in arrays:
        starts.append(starts[-1] + values.shape[0] // chunk_rows)
    columns = arrays[0].shape[1]
    half = chunk_rows // 2
    full_slot = pltpu.VMEM((slots, chunk_rows, columns), jnp.bfloat16)
    half_slot = pltpu.VMEM((slots, half, columns), jnp.bfloat16)
    moved = sum(values.size for values in arrays) * 2
    return pl.pallas_call(
        functools.partial(sum_kernel, tuple(starts), width),
        out_shape=[jax.ShapeDtypeStruct(values.shape, values.dtype) for values in arrays],
        in_specs=[pl.BlockSpec(memory_space=pl.ANY)] * len(arrays),
        out_specs=[pl.BlockSpec(memory_space=pl.ANY)] * len(arrays),
        scratch_shapes=[
            full_slot, half_slot, half_slot, half_slot, half_slot, half_slot, half_slot,
            full_slot, full_slot, full_slot, half_slot, half_slot, half_slot, half_slot, half_slot,
            pltpu.SemaphoreType.DMA((2, slots)),
            pltpu.SemaphoreType.DMA((2, 2, slots)),
            pltpu.SemaphoreType.DMA((11, slots)),
            pltpu.SemaphoreType.DMA((11, slots)),
        ],
        compiler_params=pltpu.CompilerParams(
            collective_id=0, has_side_effects=True, vmem_limit_bytes=48 * 1024 * 1024
        ),
        cost_estimate=pl.CostEstimate(flops=moved, bytes_accessed=20 * moved, transcendentals=0),
    )(*arrays)


def transpose_kernel(scale_ref, values_ref, result_ref):
    result_ref[...] = values_ref[...].astype(jnp.float32).T * scale_ref[0]


def transpose_scaled(values, scale):
    rows, columns = values.shape
    return pl.pallas_call(
        transpose_kernel,
        grid=(rows // 128,),
        in_specs=[
            pl.BlockSpec(memory_space=pltpu.SMEM),
            pl.BlockSpec((128, columns), lambda i: (i, 0)),
        ],
        out_specs=pl.BlockSpec((columns, 128), lambda i: (0, i)),
        out_shape=jax.ShapeDtypeStruct((columns, rows), jnp.float32),
        cost_estimate=pl.CostEstimate(
            flops=values.size, bytes_accessed=6 * values.size, transcendentals=0
        ),
    )(scale.reshape(1), values)


def sum_over_dp(arrays):
    depth, width = dp_layout()
    rows = [values.shape[0] for values in arrays]
    even = sum(rows) % (2 * chunk_rows) == 0 and all(row % chunk_rows == 0 for row in rows)
    if (depth, width) == (4, 2) and even:
        return kernel_sum(arrays)
    return [lax.psum(values, "dp") for values in arrays]


def tensor_masks():
    size = lax.axis_size("tensor")
    masks = []
    mask = 1
    while mask < size:
        masks.append(mask)
        mask *= 2
    return masks


def tensor_permute(values, mask):
    size = lax.axis_size("tensor")
    return lax.ppermute(values, "tensor", [(i, i ^ mask) for i in range(size)])


def sum_over_tensor(values):
    core = lax.axis_index("tensor") % 2
    keep, send = split_rows(values, core)
    total = keep + tensor_permute(send, 1)
    for mask in tensor_masks()[1:]:
        received = tensor_permute(total, mask)
        total = total + received
    return join_rows(total, tensor_permute(total, 1), core)


def scatter_step(pieces, mask):
    high = (lax.axis_index("tensor") // mask) % 2 == 1
    lower, upper = pieces[0::2], pieces[1::2]
    keep = jnp.where(high, jnp.concatenate(upper, axis=1), jnp.concatenate(lower, axis=1))
    send = jnp.where(high, jnp.concatenate(lower, axis=1), jnp.concatenate(upper, axis=1))
    received = tensor_permute(send, mask)
    return jnp.split(keep + received, len(lower), axis=1)


def scatter_over_tensor(values):
    pieces = jnp.split(values, lax.axis_size("tensor"), axis=1)
    for mask in tensor_masks():
        pieces = scatter_step(pieces, mask)
    return pieces[0]


def gather_over_tensor(values):
    member = lax.axis_index("tensor")
    pieces = [values]
    for mask in reversed(tensor_masks()):
        low = (member // mask) % 2 == 0
        joined = jnp.concatenate(pieces, axis=1) if len(pieces) > 1 else pieces[0]
        received = tensor_permute(joined, mask)
        others = jnp.split(received, len(pieces), axis=1)
        pieces = [
            piece
            for own, other in zip(pieces, others)
            for piece in (jnp.where(low, own, other), jnp.where(low, other, own))
        ]
    return jnp.concatenate(pieces, axis=1)


def sum_small(values):
    flat = jnp.concatenate([value.reshape(-1) for value in values])
    size = flat.shape[0]
    total = jnp.pad(flat, (0, -size % 1024)).reshape(-1, 128)
    for mask in tensor_masks():
        total = total + tensor_permute(total, mask)
    ends = []
    for value in values:
        ends.append((ends[-1] if ends else 0) + value.size)
    return jnp.split(total.reshape(-1)[:size], ends[:-1])


def fold_rows(values, columns):
    return jnp.concatenate(jnp.split(values, columns // values.shape[1], axis=0), axis=1)


def unfold_rows(values, columns):
    return jnp.concatenate(jnp.split(values, values.shape[1] // columns, axis=1), axis=0)


def exact_parts(value, count):
    parts = []
    for _ in range(count):
        part = value.astype(jnp.bfloat16).astype(jnp.float32)
        parts.append(part)
        value = value - part
    return parts


def lane_angles(seq_len, head_dim):
    lane = jnp.arange(head_dim)
    cosines, sines = rope_angles(
        jnp.arange(seq_len, dtype=jnp.float32), (lane // 2).astype(jnp.float32), head_dim
    )
    return cosines, jnp.where(lane % 2 == 0, -sines, sines)


def turn_lanes(values, cosines, signed_sines):
    size = values.shape[1]
    even = lax.broadcasted_iota(jnp.int32, values.shape, 1) % 2 == 0
    partner = jnp.where(even, pltpu.roll(values, size - 1, 1), pltpu.roll(values, 1, 1))
    return values * cosines + partner * signed_sines


def across(left, right, left_dim, right_dim):
    return lax.dot_general(
        left,
        right,
        (((left_dim,), (right_dim,)), ((), ())),
        preferred_element_type=jnp.float32,
    )


def keyvalue_kernel(normed_ref, weight_ref, cos_ref, sin_ref, key_ref, value_ref):
    head_dim = key_ref.shape[1]
    both = across(normed_ref[...], weight_ref[...], 1, 0)
    key_ref[...] = turn_lanes(both[:, :head_dim], cos_ref[...], sin_ref[...]).astype(jnp.bfloat16)
    value_ref[...] = both[:, head_dim:].astype(jnp.bfloat16)


def softmax_block(query, key, length, offset, scale):
    scores = across(query, key, 1, 1) * scale
    row = offset + lax.broadcasted_iota(jnp.int32, scores.shape, 0)
    col = lax.broadcasted_iota(jnp.int32, scores.shape, 1)
    scores = jnp.where((row >= col) & (col < length), scores, masked_score)
    weights = jnp.exp(scores - jnp.max(scores, axis=1, keepdims=True))
    return weights * (1.0 / jnp.sum(weights, axis=1, keepdims=True))


def forward_kernel(
    offset, scale, length_ref, latent_ref, weight_ref, key_ref, value_ref, cos_ref, sin_ref,
    query_ref, context_ref,
):
    query = turn_lanes(
        across(latent_ref[...], weight_ref[...], 1, 0), cos_ref[...], sin_ref[...]
    ).astype(jnp.bfloat16)
    query_ref[...] = query
    probability = softmax_block(query, key_ref[...], length_ref[0], offset, scale)
    context_ref[...] = across(probability.astype(jnp.bfloat16), value_ref[...], 1, 0).astype(
        jnp.bfloat16
    )


def backward_kernel(
    offset, scale, final, length_ref, query_ref, grad_ref, key_ref, value_ref, cos_ref, sin_ref,
    key_cos_ref, key_sin_ref, *refs,
):
    earlier, (query_grad_ref, sums_ref, total) = refs[:-3], refs[-3:]
    size = query_ref.shape[1]
    head = pl.program_id(0)

    @pl.when(head == 0)
    def _():
        total[...] = jnp.zeros_like(total)
        if earlier:
            total[:offset] = earlier[0][...]

    query, key = query_ref[...], key_ref[...]
    probability = softmax_block(query, key, length_ref[0], offset, scale)
    grad_probs = across(grad_ref[...], value_ref[...], 1, 1)
    inner = jnp.sum(probability * grad_probs, axis=1, keepdims=True)
    grad_scores = (scale * probability * (grad_probs - inner)).astype(jnp.bfloat16)
    query_grad_ref[...] = turn_lanes(
        across(grad_scores, key, 1, 0), cos_ref[...], -sin_ref[...]
    ).astype(jnp.bfloat16)
    total[:, :size] += across(grad_scores, query, 0, 0)
    total[:, size:] += across(probability.astype(jnp.bfloat16), grad_ref[...], 0, 0)

    @pl.when(head == pl.num_programs(0) - 1)
    def _():
        if final:
            sums_ref[:, :size] = turn_lanes(
                total[:, :size], key_cos_ref[...], -key_sin_ref[...]
            ).astype(sums_ref.dtype)
            sums_ref[:, size:] = total[:, size:].astype(sums_ref.dtype)
        else:
            sums_ref[...] = total[...]


def project_keyvalue(normed, weight, cosines, sines):
    rows, width = normed.shape
    head_dim = weight.shape[1] // 2
    block = min(256, rows)
    angle = pl.BlockSpec((block, head_dim), lambda i: (i, 0))
    return pl.pallas_call(
        keyvalue_kernel,
        grid=(rows // block,),
        in_specs=[
            pl.BlockSpec((block, width), lambda i: (i, 0)),
            pl.BlockSpec(weight.shape, lambda i: (0, 0)),
            angle,
            angle,
        ],
        out_specs=[angle, angle],
        out_shape=[jax.ShapeDtypeStruct((rows, head_dim), jnp.bfloat16)] * 2,
        cost_estimate=pl.CostEstimate(
            flops=2 * normed.size * weight.shape[1], bytes_accessed=8 << 20, transcendentals=0
        ),
    )(normed, weight, cosines, sines)


def attend(part, block, length, latent, weight, key, value, cosines, sines):
    head_dim = key.shape[1]
    rank, columns = weight.shape
    live = (part + 1) * block
    head = pl.BlockSpec((block, head_dim), lambda h: (0, h))
    fixed = pl.BlockSpec((live, head_dim), lambda h: (0, 0))
    angle = pl.BlockSpec((block, head_dim), lambda h: (part, 0))
    return pl.pallas_call(
        functools.partial(forward_kernel, part * block, 1.0 / math.sqrt(head_dim)),
        grid=(columns // head_dim,),
        in_specs=[
            pl.BlockSpec(memory_space=pltpu.SMEM),
            pl.BlockSpec((block, rank), lambda h: (part, 0)),
            pl.BlockSpec((rank, head_dim), lambda h: (0, h)),
            fixed,
            fixed,
            angle,
            angle,
        ],
        out_specs=[head, head],
        out_shape=[jax.ShapeDtypeStruct((block, columns), jnp.bfloat16)] * 2,
        cost_estimate=pl.CostEstimate(
            flops=2 * block * columns * (rank + 2 * live),
            bytes_accessed=8 << 20,
            transcendentals=block * live * columns // head_dim,
        ),
    )(length, latent, weight, key, value, cosines, sines)


def attend_back(part, block, final, length, query, grad, key, value, cosines, sines, earlier):
    head_dim = key.shape[1]
    columns = query.shape[1]
    live = (part + 1) * block
    head = pl.BlockSpec((block, head_dim), lambda h: (0, h))
    fixed = pl.BlockSpec((live, head_dim), lambda h: (0, 0))
    angle = pl.BlockSpec((block, head_dim), lambda h: (part, 0))
    both = pl.BlockSpec((live, 2 * head_dim), lambda h: (0, 0))
    specs = [pl.BlockSpec(memory_space=pltpu.SMEM), head, head, fixed, fixed, angle, angle]
    specs += [fixed, fixed] + [pl.BlockSpec(values.shape, lambda h: (0, 0)) for values in earlier]
    return pl.pallas_call(
        functools.partial(backward_kernel, part * block, 1.0 / math.sqrt(head_dim), final),
        grid=(columns // head_dim,),
        in_specs=specs,
        out_specs=[head, both],
        out_shape=[
            jax.ShapeDtypeStruct((block, columns), jnp.bfloat16),
            jax.ShapeDtypeStruct(
                (live, 2 * head_dim), jnp.bfloat16 if final else jnp.float32
            ),
        ],
        scratch_shapes=[pltpu.VMEM((live, 2 * head_dim), jnp.float32)],
        cost_estimate=pl.CostEstimate(
            flops=10 * block * columns * live,
            bytes_accessed=8 << 20,
            transcendentals=block * live * columns // head_dim,
        ),
    )(length, query, grad, key, value, cosines, sines, cosines, sines, *earlier)


def layer(
    inputs,
    teacher,
    lengths,
    gain_one,
    w_query_down,
    gain_query,
    w_query_up,
    w_keyvalue,
    w_output,
    gain_two,
    w_gate,
    w_up,
    w_down,
):
    groups = lax.axis_size("tensor")
    member = lax.axis_index("tensor")
    tokens, model_width = inputs.shape
    seq_count = lengths.shape[0]
    seq_len = tokens // seq_count
    head_dim = w_keyvalue.shape[1] // 2
    rank_local = w_query_down.shape[1]
    rank_full = w_query_up.shape[0]
    width_local = model_width // groups
    keyvalue_local = 2 * head_dim // groups
    block_rows = min(512, seq_len)
    assert seq_count == 1
    cosines, sines = lane_angles(seq_len, head_dim)
    key_live = jnp.arange(seq_len)[None, :] < lengths[:, None]
    valid_rows = key_live.reshape(tokens, 1)
    inputs_f = inputs.astype(jnp.float32)
    inverse_one = lax.rsqrt(jnp.mean(inputs_f * inputs_f, axis=-1, keepdims=True) + epsilon)
    normed = (gain_one * inputs_f * inverse_one).astype(jnp.bfloat16)
    latent = jnp.dot(normed, w_query_down, preferred_element_type=jnp.float32).astype(jnp.bfloat16)
    latent_f = latent.astype(jnp.float32)
    gain_slice = lax.dynamic_slice_in_dim(gain_query, member * rank_local, rank_local)
    latent_whole = gather_over_tensor(latent).astype(jnp.float32)
    inverse_query = lax.rsqrt(
        jnp.mean(latent_whole * latent_whole, axis=-1, keepdims=True) + epsilon
    )
    latent_normed = (gain_query * latent_whole * inverse_query).astype(jnp.bfloat16)
    key_rows, value_rows = project_keyvalue(normed, w_keyvalue, cosines, sines)
    query_parts, context_parts = [], []
    for part in range(seq_len // block_rows):
        query_part, context_part = attend(
            part, block_rows, lengths, latent_normed, w_query_up, key_rows, value_rows,
            cosines, sines,
        )
        query_parts.append(query_part)
        context_parts.append(context_part)
    context = jnp.concatenate(context_parts, axis=0)
    part_rows = seq_count * block_rows
    parts = range(len(context_parts))

    def rows_of(values, part):
        return values[part * part_rows : (part + 1) * part_rows]

    attention_parts = [
        sum_over_tensor(
            jnp.dot(
                context_parts[part], w_output, preferred_element_type=jnp.float32
            ).astype(jnp.bfloat16),
        )
        for part in parts
    ]
    residuals, inverses, normed_twos, hiddens = [], [], [], []
    gates, ups, differs, grad_outs = [], [], [], []
    for part in parts:
        attention_part = attention_parts[part]
        if part > 0:
            attention_part, hiddens[-1] = lax.optimization_barrier((attention_part, hiddens[-1]))
        residual = rows_of(inputs_f, part) + attention_part.astype(jnp.float32)
        inverse_two = lax.rsqrt(jnp.mean(residual * residual, axis=-1, keepdims=True) + epsilon)
        normed_two = (gain_two * residual * inverse_two).astype(jnp.bfloat16)
        gate_values = jnp.dot(normed_two, w_gate, preferred_element_type=jnp.float32)
        up_values = jnp.dot(normed_two, w_up, preferred_element_type=jnp.float32)
        hidden = (gate_values * jax.nn.sigmoid(gate_values) * up_values).astype(jnp.bfloat16)
        feed = jnp.dot(hidden, w_down, preferred_element_type=jnp.float32).astype(jnp.bfloat16)
        feed_share = scatter_over_tensor(feed).astype(jnp.float32)
        residual_share = lax.dynamic_slice_in_dim(residual, member * width_local, width_local, 1)
        output = (residual_share + feed_share).astype(jnp.bfloat16)
        differ = jnp.where(
            rows_of(valid_rows, part),
            output.astype(jnp.float32) - rows_of(teacher, part).astype(jnp.float32),
            0.0,
        )
        residuals.append(residual)
        inverses.append(inverse_two)
        normed_twos.append(normed_two)
        hiddens.append(hidden)
        gates.append(gate_values)
        ups.append(up_values)
        differs.append((output, differ))
        grad_outs.append(gather_over_tensor(differ.astype(jnp.bfloat16)))
    output = jnp.concatenate([pair[0] for pair in differs], axis=0)
    differ = jnp.concatenate([pair[1] for pair in differs], axis=0)
    normed_two = jnp.concatenate(normed_twos, axis=0)
    error_part = jnp.sum(differ * differ, keepdims=True).reshape(1)
    gate_grads, up_grads, part_sums = [], [], []
    for part in parts:
        gate_values, up_values = gates[part], ups[part]
        if part > 0:
            grad_outs[part], gate_grads[-1], up_grads[-1] = lax.optimization_barrier(
                (grad_outs[part], gate_grads[-1], up_grads[-1])
            )
        sigmoid_gate = jax.nn.sigmoid(gate_values)
        grad_hidden = jnp.einsum(
            "td,fd->tf", grad_outs[part], w_down, preferred_element_type=jnp.float32
        )
        gate_grad = (
            grad_hidden * up_values * sigmoid_gate * (1.0 + gate_values * (1.0 - sigmoid_gate))
        ).astype(jnp.bfloat16)
        up_grad = (grad_hidden * gate_values * sigmoid_gate).astype(jnp.bfloat16)
        gate_grads.append(gate_grad)
        up_grads.append(up_grad)
        part_sum = (
            jnp.einsum("tf,kf->tk", gate_grad, w_gate, preferred_element_type=jnp.float32)
            + jnp.einsum("tf,kf->tk", up_grad, w_up, preferred_element_type=jnp.float32)
        ).astype(jnp.bfloat16)
        part_sums.append(sum_over_tensor(part_sum))
    gate_grad = jnp.concatenate(gate_grads, axis=0)
    up_grad = jnp.concatenate(up_grads, axis=0)
    grad_w_gate = jnp.einsum("tk,tf->kf", normed_two, gate_grad, preferred_element_type=jnp.float32)
    grad_w_up = jnp.einsum("tk,tf->fk", normed_two, up_grad, preferred_element_type=jnp.float32)
    grad_w_down = sum(
        jnp.einsum("tf,td->fd", hiddens[part], grad_outs[part], preferred_element_type=jnp.float32)
        for part in parts
    )
    grad_gain_two = 0.0
    residual_lows, residual_shares, grad_contexts = [], [], []
    for part in parts:
        residual, inverse_two = residuals[part], inverses[part]
        part_sum = part_sums[part]
        if part > 0:
            part_sum, grad_contexts[-1] = lax.optimization_barrier((part_sum, grad_contexts[-1]))
        grad_normed_two = part_sum.astype(jnp.float32)
        scaled_two = gain_two * grad_normed_two
        grad_residual = (
            grad_outs[part].astype(jnp.float32)
            + inverse_two * scaled_two
            - residual * inverse_two**3 * jnp.mean(scaled_two * residual, axis=-1, keepdims=True)
        )
        grad_gain_two = grad_gain_two + jnp.sum(grad_normed_two * residual * inverse_two, axis=0)
        grad_residual_low = grad_residual.astype(jnp.bfloat16)
        residual_lows.append(grad_residual_low)
        residual_shares.append(
            lax.dynamic_slice_in_dim(grad_residual, member * width_local, width_local, 1)
        )
        grad_contexts.append(
            jnp.einsum(
                "td,cd->tc", grad_residual_low, w_output, preferred_element_type=jnp.float32
            ).astype(jnp.bfloat16)
        )
    grad_gain_two = lax.dynamic_slice_in_dim(grad_gain_two, member * width_local, width_local)
    grad_residual_low = jnp.concatenate(residual_lows, axis=0)
    residual_grad_share = jnp.concatenate(residual_shares, axis=0)
    grad_w_output = jnp.einsum(
        "tc,td->cd", context, grad_residual_low, preferred_element_type=jnp.float32
    )
    query_grads, earlier = [], []
    for part in parts:
        query_grad, keyvalue_part = attend_back(
            part, block_rows, part == parts[-1], lengths, query_parts[part], grad_contexts[part],
            key_rows, value_rows, cosines, sines, earlier,
        )
        query_grads.append(query_grad)
        earlier = [keyvalue_part]
    grad_query_pre = jnp.concatenate(query_grads, axis=0)
    grad_w_query_up = jnp.einsum(
        "tr,tc->rc", latent_normed, grad_query_pre, preferred_element_type=jnp.float32
    )
    latent_part = jnp.einsum(
        "tc,rc->tr", grad_query_pre, w_query_up, preferred_element_type=jnp.float32
    )
    grad_keyvalue = scatter_over_tensor(keyvalue_part)
    (latent_dots,) = sum_small([jnp.sum(gain_query * latent_part * latent_whole, axis=-1)])
    latent_share = scatter_over_tensor(latent_part.astype(jnp.bfloat16)).astype(jnp.float32)
    w_keyvalue_share = lax.dynamic_slice_in_dim(
        w_keyvalue, member * keyvalue_local, keyvalue_local, 1
    )
    grad_w_keyvalue = jnp.einsum(
        "tk,tc->kc", normed, grad_keyvalue, preferred_element_type=jnp.float32
    )
    scaled_latent = gain_slice * latent_share
    grad_gain_query = jnp.sum(latent_share * latent_f * inverse_query, axis=0)
    grad_latent = (
        inverse_query * scaled_latent
        - latent_f * inverse_query**3 * (latent_dots / rank_full)[:, None]
    ).astype(jnp.bfloat16)
    grad_w_query_down = jnp.einsum(
        "tk,tr->kr", normed, grad_latent, preferred_element_type=jnp.float32
    )
    normed_part = jnp.einsum(
        "tr,kr->tk", grad_latent, w_query_down, preferred_element_type=jnp.float32
    ) + jnp.einsum("tc,kc->tk", grad_keyvalue, w_keyvalue_share, preferred_element_type=jnp.float32)
    input_dots, gain_one_sums, error_part = sum_small(
        [
            jnp.sum(gain_one * normed_part * inputs_f, axis=-1),
            jnp.sum(normed_part * inputs_f * inverse_one, axis=0),
            error_part,
        ]
    )
    grad_gain_one = lax.dynamic_slice_in_dim(gain_one_sums, member * width_local, width_local)
    dp_size = lax.axis_size("dp")
    own_slot = (jnp.arange(dp_size) == lax.axis_index("dp"))[:, None]
    scalar_parts = jnp.stack(
        exact_parts(error_part[0], 3) + exact_parts(jnp.sum(lengths).astype(jnp.float32), 2)
    )
    small_row = jnp.concatenate(
        [
            grad_gain_one,
            grad_gain_query,
            grad_gain_two,
            jnp.where(own_slot, scalar_parts[None, :], 0.0).reshape(5 * dp_size),
        ]
    ).astype(jnp.bfloat16)
    small = jnp.pad(
        small_row[None, :], ((0, 2 * chunk_rows - 1), (0, model_width - small_row.shape[0]))
    )
    normed_pieces = scatter_step(
        jnp.split(normed_part.astype(jnp.bfloat16), groups, axis=1), tensor_masks()[0]
    )
    summands = [
        grad_w_down.astype(jnp.bfloat16),
        grad_w_up.astype(jnp.bfloat16),
        grad_w_output.astype(jnp.bfloat16),
        fold_rows(grad_w_query_up.astype(jnp.bfloat16), model_width),
        fold_rows(grad_w_query_down.astype(jnp.bfloat16), model_width),
        fold_rows(grad_w_keyvalue.astype(jnp.bfloat16), model_width),
        small,
    ]
    summands = lax.optimization_barrier((summands, normed_pieces))[0]
    for mask in tensor_masks()[1:]:
        normed_pieces = scatter_step(normed_pieces, mask)
    grad_normed = normed_pieces[0].astype(jnp.float32)
    dp_totals = sum_over_dp(summands)
    (
        down_total, up_total, output_total, query_up_total, query_down_total, keyvalue_total, small_total,
    ) = dp_totals
    grad_gain_one, grad_gain_query, grad_gain_two, scalar_sums = jnp.split(
        small_total[0, : small_row.shape[0]].astype(jnp.float32),
        [width_local, width_local + rank_local, 2 * width_local + rank_local],
    )
    scalar_sums = scalar_sums.reshape(dp_size, 5)
    valid_count = jnp.sum(scalar_sums[:, 3:])
    layer_loss = jnp.sum(scalar_sums[:, :3]) / (valid_count * model_width)
    grad_scale = float(tokens * dp_size) / valid_count
    grad_gain_one, grad_gain_query, grad_gain_two = (
        values * grad_scale for values in (grad_gain_one, grad_gain_query, grad_gain_two)
    )
    inputs_share = lax.dynamic_slice_in_dim(inputs_f, member * width_local, width_local, 1)
    gain_share = lax.dynamic_slice_in_dim(gain_one, member * width_local, width_local)
    scaled_one = gain_share * grad_normed
    input_grad = (
        grad_scale
        * (
            residual_grad_share
            + inverse_one * scaled_one
            - inputs_share * inverse_one**3 * (input_dots / model_width)[:, None]
        )
    ).astype(jnp.bfloat16)
    weight_grads = {}
    weight_grads["gate"] = lax.psum(grad_w_gate.astype(jnp.bfloat16), "dp")
    weight_grads["down"] = down_total
    weight_grads["output"] = output_total
    weight_grads["query_up"] = unfold_rows(query_up_total, w_query_up.shape[1])
    weight_grads["query_down"] = unfold_rows(query_down_total, rank_local)
    weight_grads["keyvalue"] = unfold_rows(keyvalue_total, keyvalue_local)
    weight_grads = {
        name: values.astype(jnp.float32) * grad_scale for name, values in weight_grads.items()
    }
    grad_w_down, grad_w_gate, grad_w_output = (
        weight_grads[name] for name in ("down", "gate", "output")
    )
    if up_total.shape[0] % 128 == 0:
        grad_w_up = transpose_scaled(up_total, grad_scale)
    else:
        grad_w_up = up_total.T.astype(jnp.float32) * grad_scale
    grad_w_query_up, grad_w_query_down, grad_w_keyvalue = (
        weight_grads[name] for name in ("query_up", "query_down", "keyvalue")
    )
    return (
        output,
        layer_loss,
        input_grad,
        grad_gain_one,
        grad_w_query_down,
        grad_gain_query,
        grad_w_query_up,
        grad_w_keyvalue,
        grad_w_output,
        grad_gain_two,
        grad_w_gate,
        grad_w_up,
        grad_w_down,
    )


def solution(mesh):
    placed = (
        P("dp", None),
        P("dp", "tensor"),
        P("dp"),
        P(),
        P(None, "tensor"),
        P(),
        P(None, "tensor"),
        P(),
        P("tensor", None),
        P(),
        P(None, "tensor"),
        P(None, "tensor"),
        P("tensor", None),
    )
    return jax.shard_map(
        layer,
        mesh=mesh,
        in_specs=placed,
        out_specs=(
            P("dp", "tensor"),
            P(),
            P("dp", "tensor"),
            P("tensor"),
            P(None, "tensor"),
            P("tensor"),
            P(None, "tensor"),
            P(None, "tensor"),
            P("tensor", None),
            P("tensor"),
            P(None, "tensor"),
            P(None, "tensor"),
            P("tensor", None),
        ),
        check_vma=False,
    )
```

time: 1470 us -> 913 us (0.62)
  waiting for transfers between devices: 978 us -> 155 us
  Pallas kernels: 0 us -> 428 us
  blocking collectives: 82.5 us -> 0 us
  matrix products: 189 us -> 136 us
  other arithmetic: 141 us -> 105 us
  starting transfers between devices: 0.78 us -> 20.6 us
    psum x3 -> x1, waiting for transfers between devices: 875 us -> 0.01 us  [layer(): weight_grads['gate'] = lax.psum(grad_w_gate.astype(jnp.bfloat16), 'dp')]
    pallas_call x0 -> x7, Pallas kernels: none -> 428 us  [the longest x1 367 us: kernel_sum(): pl.pallas_call(functools.partial(sum_kernel, tuple(starts), width), out_s...]
    ppermute x0 -> x32, waiting for transfers between devices: none -> 155 us  [tensor_permute(): return lax.ppermute(values, 'tensor', [(i, i ^ mask) for i in range(size)])]
    psum x5 -> x0, blocking collectives: 82.5 us -> none  [the longest x1 39.5 us: local(): lax.psum((jnp.sum(differ * differ), jnp.sum(lengths).astype(jnp.float32)...]
    reduce_scatter x4 -> x0, waiting for transfers between devices: 66.8 us -> none  [the longest x1 44.6 us: local(): lax.psum_scatter(jnp.dot(hidden, w_down, preferred_element_type=jnp.float...]
    dot_general x33 -> x28, matrix products: 189 us -> 136 us  [the longest x2 15.9 us: layer(): jnp.einsum('td,fd->tf', grad_outs[part], w_down, preferred_element_type=j...]
    another operation x8 -> x2, other arithmetic: 44.6 us -> 0.15 us
    all_gather x2 -> x0, waiting for transfers between devices: 36.3 us -> none  [the longest x1 35.5 us: local(): lax.all_gather(grad_share.astype(jnp.bfloat16), 'tensor', axis=1, tiled=T...]
  transfers between devices with their start and end apart: 9 -> 33, of which waited for: 7 -> 15; matrix products, arithmetic and copies ran while one was open for 8% -> 22% of each run, Pallas kernels for 0% -> 46%
where the time goes in v1:
time: 913 us; the launch traced here: 904 us
  Pallas kernels  428 us (47%)
  waiting for transfers between devices  155 us (17%)
  matrix products  136 us (15%)
  other arithmetic  105 us (12%)
  local copies, waits for them, and re-layouts  37.6 us (4%)
  between operations  21.6 us (2%)
  starting transfers between devices  20.6 us (2%)
    pallas_call x1, Pallas kernels, kernel_sum(): pl.pallas_call(functools.partial(sum_kernel, tuple(starts), width), out_s...  367 us
    ppermute x32, waiting for transfers between devices, tensor_permute(): return lax.ppermute(values, 'tensor', [(i, i ^ mask) for i in range(size)])  155 us
    mul x6, other arithmetic, layer(): values.astype(jnp.float32) * grad_scale  26.6 us
    pallas_call x2, Pallas kernels, attend_back(): pl.pallas_call(functools.partial(backward_kernel, part * block, 1.0 / mat...  22.9 us
    unnamed x279, local copies, waits for them, and re-layouts  22.2 us
    ppermute x32, starting transfers between devices, tensor_permute(): return lax.ppermute(values, 'tensor', [(i, i ^ mask) for i in range(size)])  20.6 us
    pallas_call x2, Pallas kernels, attend(): pl.pallas_call(functools.partial(forward_kernel, part * block, 1.0 / math...  20.4 us
  transfers between devices with their start and end apart: 33, of which 15 were waited for; matrix products, arithmetic and copies ran while one was open for 22% of the time, Pallas kernels for 46%

profile of v1, /device:TPU:0, one launch (start us, length us, event | category | flops | bytes accessed | tf_op | source)
XLA Modules:
  0.0 903.8 jit_solution(17010757222928881962)
XLA Ops:
  17.1 11.9 %collective-permute-done = bf16[1024,256]{1,0:T(8,128)(2,1)S(1)} collective-permute-done((bf16[1024,256]{1,0:T(8,128)(2,1)S(1)}, bf16[1024,256]{1,0:T(8,128)(2,1)S(1)}, u32[]{:S(2)}, u32[]{:S(2)}) %collective-permute-start) | collective-permute-done | bytes 524320 | tf_op jit(solution)/shard_map/ppermute | solution.py:348
  30.8 4.8 negate_select_fusion
  35.7 6.9 shard_map.228
  47.2 9.3 %shard_map.229 = (bf16[512,1024]{1,0:T(8,128)(2,1)}, bf16[512,1024]{1,0:T(8,128)(2,1)}) custom-call(s32[1]{0:T(128)} %copy.89.length_ref, bf16[1024,1024]{1,0:T(8,128)(2,1)} %fusion.15.latent_ref, bf16[1024,1024]{1,0:T(8,128)(2,1)} %weight_ref.5, bf16[1024,256]{1,0:T(8,128)(2,1)} %get-tuple-element.44.key_ref, ...), custom_call_target="tpu_custom_call" | custom-call | flops 2147483648 | bytes 8388608 | tf_op jit(solution)/shard_map/pallas_call | solution.py:541
  56.5 4.8 convolution_convert_fusion.3
  62.9 11.0 %shard_map.230 = (bf16[512,1024]{1,0:T(8,128)(2,1)}, bf16[512,1024]{1,0:T(8,128)(2,1)}) custom-call(s32[1]{0:T(128)} %copy.89.length_ref, bf16[1024,1024]{1,0:T(8,128)(2,1)} %fusion.15.latent_ref, bf16[1024,1024]{1,0:T(8,128)(2,1)} %weight_ref.5, bf16[1024,256]{1,0:T(8,128)(2,1)} %get-tuple-element.44.key_ref, ...), custom_call_target="tpu_custom_call" | custom-call | flops 3221225472 | bytes 8388608 | tf_op jit(solution)/shard_map/pallas_call | solution.py:541
  74.0 4.8 convolution_convert_fusion.2
  83.9 22.9 %collective-permute-done.3 = bf16[256,2048]{1,0:T(8,128)(2,1)S(1)} collective-permute-done((bf16[256,2048]{1,0:T(8,128)(2,1)S(1)}, bf16[256,2048]{1,0:T(8,128)(2,1)S(1)}, u32[]{:S(2)}, u32[]{:S(2)}) %collective-permute-start.3) | collective-permute-done | bytes 1048608 | tf_op jit(solution)/shard_map/ppermute | solution.py:348
  110.5 18.3 %collective-permute-done.8 = bf16[256,2048]{1,0:T(8,128)(2,1)} collective-permute-done((bf16[256,2048]{1,0:T(8,128)(2,1)S(1)}, bf16[256,2048]{1,0:T(8,128)(2,1)}, u32[]{:S(2)}, u32[]{:S(2)}) %collective-permute-start.8) | collective-permute-done | bytes 1048608 | tf_op jit(solution)/shard_map/ppermute | solution.py:348
  140.2 5.1 multiply_convert_fusion.8
  145.3 4.1 convolution_convert_fusion.5
  153.3 3.4 fusion.91
  156.7 5.1 multiply_convert_fusion.7
  161.9 3.7 convolution_convert_fusion.4
  175.6 10.5 %collective-permute-done.6 = bf16[512,512]{1,0:T(8,128)(2,1)} collective-permute-done((bf16[512,512]{1,0:T(8,128)(2,1)}, bf16[512,512]{1,0:T(8,128)(2,1)}, u32[]{:S(2)}, u32[]{:S(2)}) %collective-permute-start.6) | collective-permute-done | bytes 524320 | tf_op jit(solution)/shard_map/ppermute | solution.py:348
  186.1 10.7 %collective-permute-done.11 = bf16[512,512]{1,0:T(8,128)(2,1)} collective-permute-done((bf16[512,512]{1,0:T(8,128)(2,1)}, bf16[512,512]{1,0:T(8,128)(2,1)}, u32[]{:S(2)}, u32[]{:S(2)}) %collective-permute-start.11) | collective-permute-done | bytes 524320 | tf_op jit(solution)/shard_map/ppermute | solution.py:348
  196.8 4.0 fusion.81
  202.6 11.7 %collective-permute-done.12 = bf16[512,512]{1,0:T(8,128)(2,1)S(1)} collective-permute-done((bf16[512,512]{1,0:T(8,128)(2,1)S(1)}, bf16[512,512]{1,0:T(8,128)(2,1)S(1)}, u32[]{:S(2)}, u32[]{:S(2)}) %collective-permute-start.12) | collective-permute-done | bytes 524320 | tf_op jit(solution)/shard_map/ppermute | solution.py:348
  223.8 6.4 collective-permute-done.14
  235.1 8.3 multiply_convert_fusion.5
  243.4 5.0 fusion.93
  248.9 7.6 multiply_convert_fusion.3
  256.5 6.5 fusion.94
  263.1 5.8 add_convert_fusion.1
  271.6 3.7 add_convert_fusion.2
  278.1 8.8 convolution_convert_fusion
  286.9 7.8 fusion.92
  298.6 8.1 add_convert_fusion.refs_0_
  309.0 14.0 %collective-permute-done.17 = bf16[256,2048]{1,0:T(8,128)(2,1)S(1)} collective-permute-done((bf16[256,2048]{1,0:T(8,128)(2,1)S(1)}, bf16[256,2048]{1,0:T(8,128)(2,1)S(1)}, u32[]{:S(2)}, u32[]{:S(2)}) %collective-permute-start.17) | collective-permute-done | bytes 1048608 | tf_op jit(solution)/shard_map/ppermute | solution.py:348
  323.5 8.5 convolution_convert_fusion.1.refs_1_
  331.9 12.4 %collective-permute-done.20 = bf16[256,2048]{1,0:T(8,128)(2,1)S(1)} collective-permute-done((bf16[256,2048]{1,0:T(8,128)(2,1)S(1)}, bf16[256,2048]{1,0:T(8,128)(2,1)S(1)}, u32[]{:S(2)}, u32[]{:S(2)}) %collective-permute-start.20) | collective-permute-done | bytes 1048608 | tf_op jit(solution)/shard_map/ppermute | solution.py:348
  348.4 3.5 fusion.79
  351.9 3.4 convolution_convert_fusion.10.grad_ref
  361.8 6.3 fusion.22.refs_2_
  371.5 9.0 shard_map.231
  382.8 13.9 %shard_map.232 = (bf16[512,1024]{1,0:T(8,128)(2,1)}, bf16[1024,512]{1,0:T(8,128)(2,1)}) custom-call(s32[1]{0:T(128)} %copy.89.length_ref, bf16[512,1024]{1,0:T(8,128)(2,1)} %get-tuple-element.56.query_ref, bf16[512,1024]{1,0:T(8,128)(2,1)} %convolution_convert_fusion.9.grad_ref, bf16[1024,256]{1,0:T(8,128)(2,1)} %get-tuple-element.44.key_ref, ...), custom_call_target="tpu_custom_call" | custom-call | flops 5368709120 | bytes 8388608 | tf_op jit(solution)/shard_map/pallas_call | solution.py:573
  399.0 4.1 convolution_convert_fusion.8
  403.2 4.0 fusion.17
  419.6 6.5 collective-permute-done.27
  429.5 11.6 %collective-permute-done.23 = bf16[1024,256]{1,0:T(8,128)(2,1)S(1)} collective-permute-done((bf16[1024,256]{1,0:T(8,128)(2,1)S(1)}, bf16[1024,256]{1,0:T(8,128)(2,1)S(1)}, u32[]{:S(2)}, u32[]{:S(2)}) %collective-permute-start.23) | collective-permute-done | bytes 524320 | tf_op jit(solution)/shard_map/ppermute | solution.py:348
  445.6 4.3 multiply_reduce_fusion.1
  460.5 367.1 %shard_map.233 = (bf16[1408,2048]{1,0:T(8,128)(2,1)}, bf16[1408,2048]{1,0:T(8,128)(2,1)}, bf16[1024,2048]{1,0:T(8,128)(2,1)}, bf16[512,2048]{1,0:T(8,128)(2,1)},...) custom-call(bf16[1408,2048]{1,0:T(8,128)(2,1)} %add_convert_fusion.refs_0_, ...), custom_call_target="tpu_custom_call" | custom-call | flops 19922944 | bytes 398458880 | tf_op jit(solution)/shard_map/pallas_call | solution.py:286
  837.2 4.6 convert_multiply_fusion.2
  843.7 10.6 %shard_map.234 = f32[2048,1408]{1,0:T(8,128)} custom-call(f32[1]{0:T(128)} %bitcast.17.scale_ref, bf16[1408,2048]{1,0:T(8,128)(2,1)} %get-tuple-element.73.values_ref), custom_call_target="tpu_custom_call" | custom-call | flops 2883584 | bytes 17301504 | tf_op jit(solution)/shard_map/pallas_call | solution.py:312
  855.7 8.9 convert_multiply_fusion
  869.2 8.0 convert_multiply_fusion.1
  877.2 14.6 %collective-permute-done.31 = bf16[1024,512]{1,0:T(8,128)(2,1)} collective-permute-done((bf16[1024,512]{1,0:T(8,128)(2,1)}, bf16[1024,512]{1,0:T(8,128)(2,1)}, u32[]{:S(2)}, u32[]{:S(2)}) %collective-permute-start.31) | collective-permute-done | bytes 1048608 | tf_op jit(solution)/shard_map/ppermute | solution.py:348
  891.8 3.6 fusion.37
  (462 shorter events, 142.3 us)
Async XLA Ops:
  7.2 862.0 %all-reduce.4.cloned.1.call-start = ((), (), s32[]{:S(2)}) async-start(), calls=%async_computation | async-start | bytes 11534336 | tf_op jit(solution)/shard_map/psum | solution.py:855
  14.1 21.5 %copy-start.22 = (bf16[1024,256]{1,0:T(8,128)(2,1)}, bf16[1024,256]{1,0:T(8,128)(2,1)S(1)}, u32[]{:S(2)}) copy-start(bf16[1024,256]{1,0:T(8,128)(2,1)S(1)} %convolution_convert_fusion.11) | copy-start | bytes 1572868
  14.1 14.9 %collective-permute-start = (bf16[1024,256]{1,0:T(8,128)(2,1)S(1)}, bf16[1024,256]{1,0:T(8,128)(2,1)S(1)}, u32[]{:S(2)}, u32[]{:S(2)}) collective-permute-start(bf16[1024,256]{1,0:T(8,128)(2,1)S(1)} %convolution_convert_fusion.11), channel_id=1, source_target_pairs={{0,2},{1,3},{2,0},{3,1},{4,6},{5,7},{6,4},{7,5},{8,10},{9,11},{10,... | collective-permute-start | bytes 1572872 | tf_op jit(solution)/shard_map/ppermute | solution.py:348
  30.1 12.4 %collective-permute-start.1 = (bf16[1024,512]{1,0:T(8,128)(2,1)}, bf16[1024,512]{1,0:T(8,128)(2,1)}, u32[]{:S(2)}, u32[]{:S(2)}) collective-permute-start(bf16[1024,512]{1,0:T(8,128)(2,1)} %pad_maximum_fusion.12), channel_id=1, source_target_pairs={{0,1},{1,0},{2,3},{3,2},{4,5},{5,4},{6,7},{7,6},{8,9},{9,8},{10,11... | collective-permute-start | bytes 3145736 | tf_op jit(solution)/shard_map/ppermute | solution.py:348
  62.4 16.6 %collective-permute-start.2 = (bf16[256,2048]{1,0:T(8,128)(2,1)}, bf16[256,2048]{1,0:T(8,128)(2,1)}, u32[]{:S(2)}, u32[]{:S(2)}) collective-permute-start(bf16[256,2048]{1,0:T(8,128)(2,1)} %constant_dynamic-slice_fusion.5), channel_id=1, source_target_pairs={{0,1},{1,0},{2,3},{3,2},{4,5},{5,4},{6,7},{7,6},{8,9},{9,8},{10,11... | collective-permute-start | bytes 3145736 | tf_op jit(solution)/shard_map/ppermute | solution.py:348
  78.9 3.5 collective-permute-start.7
  80.7 26.1 %collective-permute-start.3 = (bf16[256,2048]{1,0:T(8,128)(2,1)S(1)}, bf16[256,2048]{1,0:T(8,128)(2,1)S(1)}, u32[]{:S(2)}, u32[]{:S(2)}) collective-permute-start(bf16[256,2048]{1,0:T(8,128)(2,1)S(1)} %dynamic-slice_add_fusion.3), channel_id=1, source_target_pairs={{0,2},{1,3},{2,0},{3,1},{4,6},{5,7},{6,4},{7,5},{8,10},{9,11},{10,... | collective-permute-start | bytes 3145736 | tf_op jit(solution)/shard_map/ppermute | solution.py:348
  82.9 46.0 %collective-permute-start.8 = (bf16[256,2048]{1,0:T(8,128)(2,1)S(1)}, bf16[256,2048]{1,0:T(8,128)(2,1)}, u32[]{:S(2)}, u32[]{:S(2)}) collective-permute-start(bf16[256,2048]{1,0:T(8,128)(2,1)S(1)} %dynamic-slice_add_fusion.2), channel_id=1, source_target_pairs={{0,2},{1,3},{2,0},{3,1},{4,6},{5,7},{6,4},{7,5},{8,10},{9,11},{10,... | collective-permute-start | bytes 3145736 | tf_op jit(solution)/shard_map/ppermute | solution.py:348
  107.2 23.3 %collective-permute-start.4 = (bf16[256,2048]{1,0:T(8,128)(2,1)S(1)}, bf16[256,2048]{1,0:T(8,128)(2,1)}, u32[]{:S(2)}, u32[]{:S(2)}) collective-permute-start(bf16[256,2048]{1,0:T(8,128)(2,1)S(1)} %add.252), channel_id=1, source_target_pairs={{0,1},{1,0},{2,3},{3,2},{4,5},{5,4},{6,7},{7,6},{8,9},{9,8},{10,11... | collective-permute-start | bytes 3145736 | tf_op jit(solution)/shard_map/ppermute | solution.py:348
  110.5 40.0 %copy-start.11 = (f32[1024,2048]{1,0:T(8,128)}, f32[1024,2048]{1,0:T(8,128)S(1)}, u32[]{:S(2)}) copy-start(f32[1024,2048]{1,0:T(8,128)S(1)} %convert_element_type.261) | copy-start | bytes 25165828
  130.5 2.7 collective-permute-start.9
  149.9 18.0 %collective-permute-start.5 = (bf16[512,1024]{1,0:T(8,128)(2,1)S(1)}, bf16[512,1024]{1,0:T(8,128)(2,1)}, u32[]{:S(2)}, u32[]{:S(2)}) collective-permute-start(bf16[512,1024]{1,0:T(8,128)(2,1)S(1)} %broadcast_select_fusion.4), channel_id=1, source_target_pairs={{0,1},{1,0},{2,3},{3,2},{4,5},{5,4},{6,7},{7,6},{8,9},{9,8},{10,11... | collective-permute-start | bytes 3145736 | tf_op jit(solution)/shard_map/ppermute | solution.py:348
  167.8 4.9 collective-permute-start.10
  171.0 15.1 %collective-permute-start.6 = (bf16[512,512]{1,0:T(8,128)(2,1)}, bf16[512,512]{1,0:T(8,128)(2,1)}, u32[]{:S(2)}, u32[]{:S(2)}) collective-permute-start(bf16[512,512]{1,0:T(8,128)(2,1)} %broadcast_select_fusion.28), channel_id=1, source_target_pairs={{0,2},{1,3},{2,0},{3,1},{4,6},{5,7},{6,4},{7,5},{8,10},{9,11},{10,... | collective-permute-start | bytes 1572872 | tf_op jit(solution)/shard_map/ppermute | solution.py:348
  175.3 21.5 %collective-permute-start.11 = (bf16[512,512]{1,0:T(8,128)(2,1)}, bf16[512,512]{1,0:T(8,128)(2,1)}, u32[]{:S(2)}, u32[]{:S(2)}) collective-permute-start(bf16[512,512]{1,0:T(8,128)(2,1)} %broadcast_select_fusion.27), channel_id=1, source_target_pairs={{0,2},{1,3},{2,0},{3,1},{4,6},{5,7},{6,4},{7,5},{8,10},{9,11},{10,... | collective-permute-start | bytes 1572872 | tf_op jit(solution)/shard_map/ppermute | solution.py:348
  200.8 18.3 %copy-start.45 = (f32[512,512]{1,0:T(8,128)S(1)}, f32[512,512]{1,0:T(8,128)}, u32[]{:S(2)}) copy-start(f32[512,512]{1,0:T(8,128)} %get-tuple-element.90) | copy-start | bytes 3145732
  200.8 13.5 %collective-permute-start.12 = (bf16[512,512]{1,0:T(8,128)(2,1)S(1)}, bf16[512,512]{1,0:T(8,128)(2,1)S(1)}, u32[]{:S(2)}, u32[]{:S(2)}) collective-permute-start(bf16[512,512]{1,0:T(8,128)(2,1)S(1)} %get-tuple-element.89), channel_id=1, source_target_pairs={{0,2},{1,3},{2,0},{3,1},{4,6},{5,7},{6,4},{7,5},{8,10},{9,11},{10,... | collective-permute-start | bytes 1572872 | tf_op jit(solution)/shard_map/ppermute | solution.py:348
  215.5 16.2 %collective-permute-start.13 = (bf16[512,1024]{1,0:T(8,128)(2,1)}, bf16[512,1024]{1,0:T(8,128)(2,1)}, u32[]{:S(2)}, u32[]{:S(2)}) collective-permute-start(bf16[512,1024]{1,0:T(8,128)(2,1)} %pad_maximum_fusion.18), channel_id=1, source_target_pairs={{0,1},{1,0},{2,3},{3,2},{4,5},{5,4},{6,7},{7,6},{8,9},{9,8},{10,11... | collective-permute-start | bytes 3145736 | tf_op jit(solution)/shard_map/ppermute | solution.py:348
  215.5 14.7 %collective-permute-start.14 = (bf16[512,512]{1,0:T(8,128)(2,1)}, bf16[512,512]{1,0:T(8,128)(2,1)}, u32[]{:S(2)}, u32[]{:S(2)}) collective-permute-start(bf16[512,512]{1,0:T(8,128)(2,1)} %get-tuple-element.158), channel_id=1, source_target_pairs={{0,2},{1,3},{2,0},{3,1},{4,6},{5,7},{6,4},{7,5},{8,10},{9,11},{10,... | collective-permute-start | bytes 1572872 | tf_op jit(solution)/shard_map/ppermute | solution.py:348
  231.6 16.8 %collective-permute-start.15 = (bf16[512,1024]{1,0:T(8,128)(2,1)S(1)}, bf16[512,1024]{1,0:T(8,128)(2,1)S(1)}, u32[]{:S(2)}, u32[]{:S(2)}) collective-permute-start(bf16[512,1024]{1,0:T(8,128)(2,1)S(1)} %pad_maximum_fusion.19), channel_id=1, source_target_pairs={{0,1},{1,0},{2,3},{3,2},{4,5},{5,4},{6,7},{7,6},{8,9},{9,8},{10,11... | collective-permute-start | bytes 3145736 | tf_op jit(solution)/shard_map/ppermute | solution.py:348
  248.4 14.6 %slice-start.12 = ((s8[5767168]{0:T(1024)(128)(4,1)}), s8[4194304]{0:T(1024)(128)(4,1)S(1)}, s32[]{:S(2)}) async-start(s8[5767168]{0:T(1024)(128)(4,1)} %bitcast.95), calls=%async_computation.13 | async-start | bytes 8388608
  248.9 14.1 %slice-start.13 = ((s8[5767168]{0:T(1024)(128)(4,1)}), s8[1572864]{0:T(1024)(128)(4,1)S(1)}, s32[]{:S(2)}) async-start(s8[5767168]{0:T(1024)(128)(4,1)} %bitcast.95), calls=%async_computation.14 | async-start | bytes 3145728
  256.5 15.0 %slice-start.14 = ((s8[5767168]{0:T(1024)(128)(4,1)}), s8[4194304]{0:T(1024)(128)(4,1)S(1)}, s32[]{:S(2)}) async-start(s8[5767168]{0:T(1024)(128)(4,1)} %bitcast.97), calls=%async_computation.15 | async-start | bytes 8388608
  271.4 35.2 %collective-permute-start.19 = (bf16[256,2048]{1,0:T(8,128)(2,1)}, bf16[256,2048]{1,0:T(8,128)(2,1)}, u32[]{:S(2)}, u32[]{:S(2)}) collective-permute-start(bf16[256,2048]{1,0:T(8,128)(2,1)} %constant_dynamic-slice_fusion.2), channel_id=1, source_target_pairs={{0,1},{1,0},{2,3},{3,2},{4,5},{5,4},{6,7},{7,6},{8,9},{9,8},{10,11... | collective-permute-start | bytes 3145736 | tf_op jit(solution)/shard_map/ppermute | solution.py:348
  277.7 17.1 %collective-permute-start.16 = (bf16[256,2048]{1,0:T(8,128)(2,1)}, bf16[256,2048]{1,0:T(8,128)(2,1)}, u32[]{:S(2)}, u32[]{:S(2)}) collective-permute-start(bf16[256,2048]{1,0:T(8,128)(2,1)} %constant_dynamic-slice_fusion.3), channel_id=1, source_target_pairs={{0,1},{1,0},{2,3},{3,2},{4,5},{5,4},{6,7},{7,6},{8,9},{9,8},{10,11... | collective-permute-start | bytes 3145736 | tf_op jit(solution)/shard_map/ppermute | solution.py:348
  296.9 26.1 %collective-permute-start.17 = (bf16[256,2048]{1,0:T(8,128)(2,1)S(1)}, bf16[256,2048]{1,0:T(8,128)(2,1)S(1)}, u32[]{:S(2)}, u32[]{:S(2)}) collective-permute-start(bf16[256,2048]{1,0:T(8,128)(2,1)S(1)} %dynamic-slice_add_fusion.1), channel_id=1, source_target_pairs={{0,2},{1,3},{2,0},{3,1},{4,6},{5,7},{6,4},{7,5},{8,10},{9,11},{10,... | collective-permute-start | bytes 3145736 | tf_op jit(solution)/shard_map/ppermute | solution.py:348
  298.5 24.9 %copy-start.93 = (bf16[512,1408]{1,0:T(8,128)(2,1)S(1)}, bf16[512,1408]{1,0:T(8,128)(2,1)}, u32[]{:S(2)}) copy-start(bf16[512,1408]{1,0:T(8,128)(2,1)} %get-tuple-element.101) | copy-start | bytes 4325380
  306.7 16.8 %copy-start.48 = (bf16[512,2048]{1,0:T(8,128)(2,1)S(1)}, bf16[512,2048]{1,0:T(8,128)(2,1)}, u32[]{:S(2)}) copy-start(bf16[512,2048]{1,0:T(8,128)(2,1)} %copy-done.46) | copy-start | bytes 6291460
  306.7 16.8 %copy-start.51 = (bf16[512,2048]{1,0:T(8,128)(2,1)S(1)}, bf16[512,2048]{1,0:T(8,128)(2,1)}, u32[]{:S(2)}) copy-start(bf16[512,2048]{1,0:T(8,128)(2,1)} %copy-done.49) | copy-start | bytes 6291460
  306.7 16.8 %copy-start.92 = (bf16[512,1408]{1,0:T(8,128)(2,1)S(1)}, bf16[512,1408]{1,0:T(8,128)(2,1)}, u32[]{:S(2)}) copy-start(bf16[512,1408]{1,0:T(8,128)(2,1)} %get-tuple-element.51) | copy-start | bytes 4325380
  308.5 35.9 %collective-permute-start.20 = (bf16[256,2048]{1,0:T(8,128)(2,1)S(1)}, bf16[256,2048]{1,0:T(8,128)(2,1)S(1)}, u32[]{:S(2)}, u32[]{:S(2)}) collective-permute-start(bf16[256,2048]{1,0:T(8,128)(2,1)S(1)} %dynamic-slice_add_fusion), channel_id=1, source_target_pairs={{0,2},{1,3},{2,0},{3,1},{4,6},{5,7},{6,4},{7,5},{8,10},{9,11},{10,... | collective-permute-start | bytes 3145736 | tf_op jit(solution)/shard_map/ppermute | solution.py:348
  323.3 21.5 %collective-permute-start.18 = (bf16[256,2048]{1,0:T(8,128)(2,1)S(1)}, bf16[256,2048]{1,0:T(8,128)(2,1)S(1)}, u32[]{:S(2)}, u32[]{:S(2)}) collective-permute-start(bf16[256,2048]{1,0:T(8,128)(2,1)S(1)} %add.272), channel_id=1, source_target_pairs={{0,1},{1,0},{2,3},{3,2},{4,5},{5,4},{6,7},{7,6},{8,9},{9,8},{10,11... | collective-permute-start | bytes 3145736 | tf_op jit(solution)/shard_map/ppermute | solution.py:348
  344.8 10.5 %collective-permute-start.21 = (bf16[256,2048]{1,0:T(8,128)(2,1)S(1)}, bf16[256,2048]{1,0:T(8,128)(2,1)S(1)}, u32[]{:S(2)}, u32[]{:S(2)}) collective-permute-start(bf16[256,2048]{1,0:T(8,128)(2,1)S(1)} %add.277), channel_id=1, source_target_pairs={{0,1},{1,0},{2,3},{3,2},{4,5},{5,4},{6,7},{7,6},{8,9},{9,8},{10,11... | collective-permute-start | bytes 3145736 | tf_op jit(solution)/shard_map/ppermute | solution.py:348
  382.8 16.1 %copy-start.64 = (bf16[1024,1024]{1,0:T(8,128)(2,1)S(1)}, bf16[1024,1024]{1,0:T(8,128)(2,1)}, u32[]{:S(2)}) copy-start(bf16[1024,1024]{1,0:T(8,128)(2,1)} %fusion.15.latent_ref) | copy-start | bytes 6291460
  408.9 8.8 collective-permute-start.26
  412.8 3.0 collective-permute-start.24
  415.9 3.7 collective-permute-start.25
  418.0 8.0 collective-permute-start.27
  418.4 9.3 %collective-permute-start.22 = (bf16[1024,512]{1,0:T(8,128)(2,1)S(1)}, bf16[1024,512]{1,0:T(8,128)(2,1)S(1)}, u32[]{:S(2)}, u32[]{:S(2)}) collective-permute-start(bf16[1024,512]{1,0:T(8,128)(2,1)S(1)} %broadcast_select_fusion.2), channel_id=1, source_target_pairs={{0,1},{1,0},{2,3},{3,2},{4,5},{5,4},{6,7},{7,6},{8,9},{9,8},{10,11... | collective-permute-start | bytes 3145736 | tf_op jit(solution)/shard_map/ppermute | solution.py:348
  428.2 12.9 %collective-permute-start.23 = (bf16[1024,256]{1,0:T(8,128)(2,1)S(1)}, bf16[1024,256]{1,0:T(8,128)(2,1)S(1)}, u32[]{:S(2)}, u32[]{:S(2)}) collective-permute-start(bf16[1024,256]{1,0:T(8,128)(2,1)S(1)} %broadcast_select_fusion.14), channel_id=1, source_target_pairs={{0,2},{1,3},{2,0},{3,1},{4,6},{5,7},{6,4},{7,5},{8,10},{9,11},{10,... | collective-permute-start | bytes 1572872 | tf_op jit(solution)/shard_map/ppermute | solution.py:348
  450.9 1.2 collective-permute-start.28
  452.8 3.8 collective-permute-start.29
  455.2 409.4 %collective-permute-start.30 = (bf16[1024,1024]{1,0:T(8,128)(2,1)}, bf16[1024,1024]{1,0:T(8,128)(2,1)}, u32[]{:S(2)}, u32[]{:S(2)}) collective-permute-start(bf16[1024,1024]{1,0:T(8,128)(2,1)} %broadcast_select_fusion), channel_id=1, source_target_pairs={{0,1},{1,0},{2,3},{3,2},{4,5},{5,4},{6,7},{7,6},{8,9},{9,8},{10,11... | collective-permute-start | bytes 6291464 | tf_op jit(solution)/shard_map/ppermute | solution.py:348
  868.0 23.8 %copy-start.77 = (f32[1024]{0:T(1024)S(1)}, f32[1024]{0:T(1024)}, u32[]{:S(2)}) copy-start(f32[1024]{0:T(1024)} %get-tuple-element.167) | copy-start | bytes 12292
  868.0 23.8 %copy-start.80 = (f32[512]{0:T(512)S(1)}, f32[512]{0:T(512)}, u32[]{:S(2)}) copy-start(f32[512]{0:T(512)} %dynamic_slice.70) | copy-start | bytes 6148
  868.0 23.8 %collective-permute-start.31 = (bf16[1024,512]{1,0:T(8,128)(2,1)}, bf16[1024,512]{1,0:T(8,128)(2,1)}, u32[]{:S(2)}, u32[]{:S(2)}) collective-permute-start(bf16[1024,512]{1,0:T(8,128)(2,1)} %broadcast_select_fusion.1), channel_id=1, source_target_pairs={{0,2},{1,3},{2,0},{3,1},{4,6},{5,7},{6,4},{7,5},{8,10},{9,11},{10,... | collective-permute-start | bytes 3145736 | tf_op jit(solution)/shard_map/ppermute | solution.py:348
  869.2 22.6 %copy-start.43 = (f32[512,512]{1,0:T(8,128)S(1)}, f32[512,512]{1,0:T(8,128)}, u32[]{:S(2)}) copy-start(f32[512,512]{1,0:T(8,128)} %constant_dynamic-slice_fusion.1) | copy-start | bytes 3145732
  869.2 22.6 %copy-start.44 = (f32[512,512]{1,0:T(8,128)S(1)}, f32[512,512]{1,0:T(8,128)}, u32[]{:S(2)}) copy-start(f32[512,512]{1,0:T(8,128)} %constant_dynamic-slice_fusion) | copy-start | bytes 3145732
  (102 other events, 500.8 us)
Sparse Core Ops, SparseCore 0:
  287.0 216.1 all-reduce.3
